TPU v7x, 256 devices: a whole 4x4x8 slice. The times are simulated.
256 devices in a mesh: ctx: 32 (over x, z_lo, core), head: 8 (over z_hi, y).
Axes of the slice: x: 4, y: 4, z: 8 (z_hi: 2, z_lo: 4; z = z_hi * 4 + z_lo), core: 2. Of those that a mesh axis runs over, the one named last changes fastest.
Arguments:
- absorbed_query: bfloat16 [64, 128, 576], P('ctx', 'head'), may hold values from -20 to 20
- index_query: bfloat16 [64, 64, 128], P('ctx', 'head'), may hold values from -20 to 20
- index_weight: bfloat16 [64, 64], P('ctx', 'head'), may hold values from -2 to 2
- kv_cache: bfloat16 [131072, 576], P('ctx'), may hold values from -4 to 4
- index_keys: bfloat16 [131072, 128], P('ctx'), may hold values from -4 to 4
- lengths: int32 [64], replicated, may hold values from 32768 to 131072
Outputs:
- target: float32 [64, 131072], P('head', 'ctx')
- gradient: float32 [64, 131072], P('head', 'ctx')
All inputs are finite; a program needn't handle non-finite values.
Results may differ from a plain program's by a relative error of at most 0.0003.
Values may be sent and summed in bfloat16 or wider, within the bound.
A program may use at most 128 MiB of HBM per device.

v0:
```python
import jax
import jax.numpy as jnp
from jax import lax
from jax.sharding import PartitionSpec as P

attention_scale = 192.0 ** (-0.5)
far_below = -1e30


def side_by_side(arrays, axis, dim, along):
    columns = [a.reshape(*a.shape[:along], -1) for a in arrays]
    both = jnp.concatenate(columns, axis=along)
    result, at, finished = (lax.all_gather(both, axis, axis=dim, tiled=True), 0, [])
    for a, column in zip(arrays, columns):
        piece = result[..., at : at + column.shape[along]]
        finished.append(piece.reshape(*piece.shape[:along], *a.shape[along:]))
        at += column.shape[along]
    return tuple(finished)


def sent_together(arrays, axis, split_dim, concat_dim, along):
    columns = [a.reshape(*a.shape[:along], -1) for a in arrays]
    both = jnp.concatenate(columns, axis=along)
    result, at, finished = (
        lax.all_to_all(both, axis, split_axis=split_dim, concat_axis=concat_dim, tiled=True),
        0,
        [],
    )
    for a, column in zip(arrays, columns):
        piece = result[..., at : at + column.shape[along]]
        finished.append(piece.reshape(*piece.shape[:along], *a.shape[along:]))
        at += column.shape[along]
    return tuple(finished)


def from_everyone(x, axis):
    copies = jnp.broadcast_to(x, (lax.axis_size(axis), *x.shape))
    return lax.all_to_all(copies, axis, split_axis=0, concat_axis=0, tiled=True)


def all_in_one(x, axis):
    leaves = jax.tree.leaves(x)
    turns = sorted(range(len(leaves)), key=lambda k: -leaves[k].size)
    width = (1, *leaves[turns[0]].shape)[-1]
    lines = [
        jnp.pad(leaves[k].reshape(-1), (0, -leaves[k].size % width)).reshape(-1, width)
        for k in turns
    ]
    both, at, found = (from_everyone(jnp.concatenate(lines), axis), 0, {})
    for k, line in zip(turns, lines):
        piece = both[:, at : at + len(line)].reshape(len(both), -1)
        found[k] = piece[:, : leaves[k].size].reshape(-1, *leaves[k].shape)
        at += len(line)
    numbers = iter(range(len(leaves)))
    return jax.tree.map(lambda _: found[next(numbers)], x)


def joined_by_halves(pieces, combine):
    while len(jax.tree.leaves(pieces)[0]) > 1:
        pieces = jax.vmap(combine)(
            *(jax.tree.map(lambda part: part[side::2], pieces) for side in (0, 1))
        )
    return jax.tree.map(lambda part: part[0], pieces)


def merged(x, axis, combine):
    pieces = all_in_one(x, axis)
    return joined_by_halves(pieces, combine)


def block_scores(
    flat_query, kv_cache, row_lengths, key_start, block_index, block_keys, row_count, head_count
):
    cached = lax.dynamic_slice_in_dim(kv_cache, block_index * block_keys, block_keys, 0)
    scores = (
        jnp.einsum("qd,kd->qk", flat_query, cached, preferred_element_type=jnp.float32)
        * attention_scale
    )
    scores = scores.reshape(row_count, head_count, block_keys)
    key_index = key_start + block_index * block_keys + jnp.arange(block_keys, dtype=jnp.int32)
    visible = key_index[None, :] < row_lengths[:, None]
    return jnp.where(visible[:, None, :], scores, -jnp.inf)


def first_sweep(queries, idx_query, idx_weight, kv_cache, index_keys, row_lengths, key_start):
    row_count, head_count, latent_width = queries.shape
    ctx_keys = kv_cache.shape[0]
    block_keys = min(1024, ctx_keys)
    flat_query = queries.reshape(row_count * head_count, latent_width)
    weight_full = idx_weight.astype(jnp.float32)
    index_scale = idx_query.shape[-1] ** (-0.5)

    def advance(block_index, carry):
        att_max, att_total, logits, kept = carry
        scores = block_scores(
            flat_query,
            kv_cache,
            row_lengths,
            key_start,
            block_index,
            block_keys,
            row_count,
            head_count,
        )
        kept = lax.dynamic_update_slice_in_dim(kept, scores, block_index * block_keys, 2)
        new_max = jnp.maximum(att_max, jnp.max(scores, axis=-1))
        att_total = att_total * jnp.exp(att_max - new_max) + jnp.sum(
            jnp.exp(scores - new_max[..., None]), axis=-1
        )
        idx_cached = lax.dynamic_slice_in_dim(index_keys, block_index * block_keys, block_keys, 0)
        inner = jnp.einsum("rgd,kd->rgk", idx_query, idx_cached, preferred_element_type=jnp.float32)
        piece = (
            jnp.einsum(
                "rg,rgk->rk", weight_full, jnp.maximum(inner, 0.0), precision=lax.Precision.HIGHEST
            )
            * index_scale
        )
        logits = lax.dynamic_update_slice_in_dim(logits, piece, block_index * block_keys, 1)
        return (new_max, att_total, logits, kept)

    start = (
        jnp.full((row_count, head_count), far_below, jnp.float32),
        jnp.zeros((row_count, head_count), jnp.float32),
        jnp.zeros((row_count, ctx_keys), jnp.float32),
        jnp.zeros((row_count, head_count, ctx_keys), jnp.float32),
    )
    return lax.fori_loop(0, ctx_keys // block_keys, advance, start)


def second_sweep(kept, att_max, att_total):
    weights = jnp.exp(kept - att_max[..., None]) / att_total[..., None]
    return jnp.sum(weights, axis=1)


def combine_pairs(first, second):
    outputs = []
    for place in range(0, len(first), 2):
        larger = jnp.maximum(first[place], second[place])
        total = first[place + 1] * jnp.exp(first[place] - larger) + second[place + 1] * jnp.exp(
            second[place] - larger
        )
        outputs.append(larger)
        outputs.append(total)
    return tuple(outputs)


def body(absorbed_query, index_query, index_weight, kv_cache, index_keys, lengths):
    gathered = side_by_side((absorbed_query, index_query, index_weight), "ctx", 0, 1)
    ctx_keys = kv_cache.shape[0]
    key_start = lax.axis_index("ctx") * ctx_keys
    keys_total = ctx_keys * lax.axis_size("ctx")
    heads_total = absorbed_query.shape[1] * lax.axis_size("head")
    own_rows = absorbed_query.shape[0] * lax.axis_size("ctx") // lax.axis_size("head")
    own_lengths = lax.dynamic_slice_in_dim(lengths, lax.axis_index("head") * own_rows, own_rows)
    queries, idx_query, idx_weight = (
        lax.all_to_all(gathered[0], "head", split_axis=0, concat_axis=1, tiled=True),
        *sent_together((gathered[1], gathered[2]), "head", 0, 1, 2),
    )
    att_max, att_total, logits, kept = first_sweep(
        queries, idx_query, idx_weight, kv_cache, index_keys, own_lengths, key_start
    )
    key_index = key_start + jnp.arange(ctx_keys, dtype=jnp.int32)
    logits = jnp.where(key_index[None, :] < own_lengths[:, None], logits, -jnp.inf)
    idx_max = jnp.maximum(jnp.max(logits, axis=-1), far_below)
    idx_total = jnp.sum(jnp.exp(logits - idx_max[:, None]), axis=-1)
    att_max, att_total, idx_max, idx_total = merged(
        (att_max, att_total, idx_max, idx_total), "ctx", combine_pairs
    )
    summed = second_sweep(kept, att_max, att_total)
    summed = summed / heads_total
    predicted = jnp.exp(logits - idx_max[:, None]) / idx_total[:, None]
    return (keys_total * summed, keys_total * (predicted - summed))


def solution(mesh):
    return jax.shard_map(
        body,
        mesh=mesh,
        in_specs=(
            P("ctx", "head", None),
            P("ctx", "head", None),
            P("ctx", "head"),
            P("ctx", None),
            P("ctx", None),
            P(),
        ),
        out_specs=(P("head", "ctx"), P("head", "ctx")),
        check_vma=False,
    )
```

profile of v0, /device:TPU:1, one launch (start us, length us, event | category | flops | bytes accessed | tf_op | source)
XLA Modules:
  0.0 230.9 jit_solution(8754433603944475248)
XLA Ops:
  10.1 63.4 %all-gather.3.cloned.1.call-done = bf16[32,2,10248]{2,1,0:T(2,128)(2,1)} async-done(((bf16[1,2,10248]{2,1,0:T(2,128)(2,1)}), bf16[32,2,10248]{2,1,0:T(2,128)(2,1)}) %all-gather.3.cloned.1.call-update) | async-done | bytes 1311760 | tf_op jit(solution)/shard_map/all_gather | solution.py:13
  73.6 2.1 reshape.119
  77.0 7.7 %all-to-all-start.1 = ((bf16[64,8,129]{2,1,0:T(8,128)(2,1)}), bf16[64,8,129]{2,1,0:T(8,128)(2,1)S(1)}, u32[]{:S(2)}, u32[]{:S(2)}) async-start(bf16[64,8,129]{2,1,0:T(8,128)(2,1)} %pad_maximum_fusion), calls=%async_computation.1 | async-start | bytes 524288 | tf_op jit(solution)/shard_map/all_to_all | solution.py:25
  84.7 1.9 reshape.109
  86.7 8.1 %all-to-all-done.1 = bf16[64,8,129]{2,1,0:T(8,128)(2,1)S(1)} async-done(((bf16[64,8,129]{2,1,0:T(8,128)(2,1)}), bf16[64,8,129]{2,1,0:T(8,128)(2,1)S(1)}, u32[]{:S(2)}, u32[]{:S(2)}) %all-to-all-start.1) | async-done | bytes 132128 | tf_op jit(solution)/shard_map/all_to_all | solution.py:25
  94.7 3.8 %all-to-all-start = ((bf16[64,16,576]{2,1,0:T(8,128)(2,1)}), bf16[64,16,576]{2,1,0:T(8,128)(2,1)S(1)}, u32[]{:S(2)}, u32[]{:S(2)}) async-start(bf16[64,16,576]{2,1,0:T(8,128)(2,1)} %reshape.109), calls=%async_computation | async-start | bytes 2621440 | tf_op jit(solution)/shard_map/all_to_all | solution.py:156
  98.8 18.6 %all-to-all-done = bf16[64,16,576]{2,1,0:T(8,128)(2,1)S(1)} async-done(((bf16[64,16,576]{2,1,0:T(8,128)(2,1)}), bf16[64,16,576]{2,1,0:T(8,128)(2,1)S(1)}, u32[]{:S(2)}, u32[]{:S(2)}) %all-to-all-start) | async-done | bytes 1179680 | tf_op jit(solution)/shard_map/all_to_all | solution.py:156
  117.6 7.8 %broadcast_in_dim.67 = f32[8,128,4096]{2,1,0:T(8,128)} broadcast(f32[]{:T(128)} %constant.77.clone.1), dimensions={} | broadcast | bytes 16777220 | tf_op jit(solution)/shard_map/broadcast_in_dim | solution.py:125
  125.4 53.8 %while.20 = (s32[]{:T(128)}, f32[8,128]{1,0:T(8,128)S(1)}, f32[8,128]{1,0:T(8,128)S(1)}, f32[8,4096]{1,0:T(8,128)S(1)}, f32[8,128,4096]{2,1,0:T(8,128)}, /*index...) while((s32[]{:T(128)}, f32[8,128]{1,0:T(8,128)S(1)}, ...), condition=%wide.region_3.4_spmd.clone, body=%wide.region_0.3_spmd.clone.sunk | while | flops 1356358656 | bytes 40700208 | solution.py:127
  125.5 5.0 %fusion.38 = (f32[1024]{0:T(1024)S(1)}, f32[1024,1024]{0,1:T(8,128)}) fusion(pred[8,1024]{1,0:T(8,128)(4,1)S(1)} %broadcast_compare_fusion.2, bf16[1024,576]{1,0:T(8,128)(2,1)S(1)} %get-tuple-element.430, bf16[4096,576]{0,1:T(8,128)(2,1)} %get-tuple-element.429, s32[]{:T(128)S(6)} %select_n.58), kind=kOutput, calls=%fused_computation.3.clone.1 | convolution fusion | flops 1211104256 | bytes 6565892 | tf_op jit(solution)/shard_map/while/body/eval_jaxpr/qd,kd->qk/dot_general | solution.py:76
  130.5 3.2 %exponential_reduce_fusion.3 = f32[1024]{0:T(1024)S(1)} fusion(f32[1024,1024]{0,1:T(8,128)} %get-tuple-element.389, f32[1024]{0:T(1024)S(1)} %fusion.39, pred[8,1024]{1,0:T(8,128)(4,1)S(1)} %broadcast_compare_fusion.2), kind=kLoop, calls=%fused_computation.2.clone.1 | loop fusion | flops 3144704 | bytes 4210688 | tf_op jit(solution)/shard_map/while/body/eval_jaxpr/reduce_sum | solution.py:107
  133.7 1.4 fusion.40
  136.4 2.4 %select_dynamic-update-slice_fusion.2 = f32[8,128,4096]{2,1,0:T(8,128)} fusion(f32[8,128,4096]{2,1,0:T(8,128)} %get-tuple-element.410, s32[]{:T(128)S(6)} %select_n.58, f32[8,128,1024]{2,1,0:T(8,128)S(1)} %bitcast.113, pred[8,1024]{1,0:T(8,128)(4,1)S(1)} %broadcast_compare_fusion.2), kind=kLoop, calls=%fused_computation.1.clone.1 | loop fusion | flops 1048576 | bytes 8396804 | tf_op jit(solution)/shard_map/while/body/eval_jaxpr/dynamic_update_slice | solution.py:105
  138.9 5.0 %fusion.38 = (f32[1024]{0:T(1024)S(1)}, f32[1024,1024]{0,1:T(8,128)}) fusion(pred[8,1024]{1,0:T(8,128)(4,1)S(1)} %broadcast_compare_fusion.2, bf16[1024,576]{1,0:T(8,128)(2,1)S(1)} %get-tuple-element.430, bf16[4096,576]{0,1:T(8,128)(2,1)} %get-tuple-element.429, s32[]{:T(128)S(6)} %select_n.58), kind=kOutput, calls=%fused_computation.3.clone.1 | convolution fusion | flops 1211104256 | bytes 6565892 | tf_op jit(solution)/shard_map/while/body/eval_jaxpr/qd,kd->qk/dot_general | solution.py:76
  143.9 3.2 %exponential_reduce_fusion.3 = f32[1024]{0:T(1024)S(1)} fusion(f32[1024,1024]{0,1:T(8,128)} %get-tuple-element.389, f32[1024]{0:T(1024)S(1)} %fusion.39, pred[8,1024]{1,0:T(8,128)(4,1)S(1)} %broadcast_compare_fusion.2), kind=kLoop, calls=%fused_computation.2.clone.1 | loop fusion | flops 3144704 | bytes 4210688 | tf_op jit(solution)/shard_map/while/body/eval_jaxpr/reduce_sum | solution.py:107
  149.9 2.4 %select_dynamic-update-slice_fusion.2 = f32[8,128,4096]{2,1,0:T(8,128)} fusion(f32[8,128,4096]{2,1,0:T(8,128)} %get-tuple-element.410, s32[]{:T(128)S(6)} %select_n.58, f32[8,128,1024]{2,1,0:T(8,128)S(1)} %bitcast.113, pred[8,1024]{1,0:T(8,128)(4,1)S(1)} %broadcast_compare_fusion.2), kind=kLoop, calls=%fused_computation.1.clone.1 | loop fusion | flops 1048576 | bytes 8396804 | tf_op jit(solution)/shard_map/while/body/eval_jaxpr/dynamic_update_slice | solution.py:105
  152.3 5.0 %fusion.38 = (f32[1024]{0:T(1024)S(1)}, f32[1024,1024]{0,1:T(8,128)}) fusion(pred[8,1024]{1,0:T(8,128)(4,1)S(1)} %broadcast_compare_fusion.2, bf16[1024,576]{1,0:T(8,128)(2,1)S(1)} %get-tuple-element.430, bf16[4096,576]{0,1:T(8,128)(2,1)} %get-tuple-element.429, s32[]{:T(128)S(6)} %select_n.58), kind=kOutput, calls=%fused_computation.3.clone.1 | convolution fusion | flops 1211104256 | bytes 6565892 | tf_op jit(solution)/shard_map/while/body/eval_jaxpr/qd,kd->qk/dot_general | solution.py:76
  157.4 3.2 %exponential_reduce_fusion.3 = f32[1024]{0:T(1024)S(1)} fusion(f32[1024,1024]{0,1:T(8,128)} %get-tuple-element.389, f32[1024]{0:T(1024)S(1)} %fusion.39, pred[8,1024]{1,0:T(8,128)(4,1)S(1)} %broadcast_compare_fusion.2), kind=kLoop, calls=%fused_computation.2.clone.1 | loop fusion | flops 3144704 | bytes 4210688 | tf_op jit(solution)/shard_map/while/body/eval_jaxpr/reduce_sum | solution.py:107
  163.3 2.4 %select_dynamic-update-slice_fusion.2 = f32[8,128,4096]{2,1,0:T(8,128)} fusion(f32[8,128,4096]{2,1,0:T(8,128)} %get-tuple-element.410, s32[]{:T(128)S(6)} %select_n.58, f32[8,128,1024]{2,1,0:T(8,128)S(1)} %bitcast.113, pred[8,1024]{1,0:T(8,128)(4,1)S(1)} %broadcast_compare_fusion.2), kind=kLoop, calls=%fused_computation.1.clone.1 | loop fusion | flops 1048576 | bytes 8396804 | tf_op jit(solution)/shard_map/while/body/eval_jaxpr/dynamic_update_slice | solution.py:105
  165.8 5.0 %fusion.38 = (f32[1024]{0:T(1024)S(1)}, f32[1024,1024]{0,1:T(8,128)}) fusion(pred[8,1024]{1,0:T(8,128)(4,1)S(1)} %broadcast_compare_fusion.2, bf16[1024,576]{1,0:T(8,128)(2,1)S(1)} %get-tuple-element.430, bf16[4096,576]{0,1:T(8,128)(2,1)} %get-tuple-element.429, s32[]{:T(128)S(6)} %select_n.58), kind=kOutput, calls=%fused_computation.3.clone.1 | convolution fusion | flops 1211104256 | bytes 6565892 | tf_op jit(solution)/shard_map/while/body/eval_jaxpr/qd,kd->qk/dot_general | solution.py:76
  170.8 3.2 %exponential_reduce_fusion.3 = f32[1024]{0:T(1024)S(1)} fusion(f32[1024,1024]{0,1:T(8,128)} %get-tuple-element.389, f32[1024]{0:T(1024)S(1)} %fusion.39, pred[8,1024]{1,0:T(8,128)(4,1)S(1)} %broadcast_compare_fusion.2), kind=kLoop, calls=%fused_computation.2.clone.1 | loop fusion | flops 3144704 | bytes 4210688 | tf_op jit(solution)/shard_map/while/body/eval_jaxpr/reduce_sum | solution.py:107
  176.7 2.5 %select_dynamic-update-slice_fusion.2 = f32[8,128,4096]{2,1,0:T(8,128)} fusion(f32[8,128,4096]{2,1,0:T(8,128)} %get-tuple-element.410, s32[]{:T(128)S(6)} %select_n.58, f32[8,128,1024]{2,1,0:T(8,128)S(1)} %bitcast.113, pred[8,1024]{1,0:T(8,128)(4,1)S(1)} %broadcast_compare_fusion.2), kind=kLoop, calls=%fused_computation.1.clone.1 | loop fusion | flops 1048576 | bytes 8396804 | tf_op jit(solution)/shard_map/while/body/eval_jaxpr/dynamic_update_slice | solution.py:105
  179.7 35.4 %all_to_all.38 = f32[32,18,128]{2,1,0:T(8,128)S(1)} all-to-all(f32[32,18,128]{2,1,0:T(8,128)S(1)} %broadcast_in_dim.69), channel_id=1, replica_groups=mesh['ctx'=32,'head'=8] {'ctx'}, dimensions={0} | all-to-all | bytes 589824 | tf_op jit(solution)/shard_map/all_to_all | solution.py:38
  215.6 7.7 %fusion.13 = f32[8,4096]{1,0:T(8,128)S(1)} fusion(f32[8,128,4096]{2,1,0:T(8,128)} %get-tuple-element.204, f32[8,128]{1,0:T(8,128)S(1)} %get-tuple-element.308, f32[8,128]{1,0:T(8,128)S(1)} %get-tuple-element.307), kind=kLoop, calls=%fused_computation.24 | loop fusion | flops 12550144 | bytes 16916480 | tf_op jit(solution)/shard_map/reduce_sum | solution.py:132
  (96 shorter events, 16.0 us)
Async XLA Ops:
  7.2 66.4 %all-gather.3.cloned.1.call-start = ((), (), s32[]{:S(2)}) async-start(), calls=%async_computation.3 | async-start | bytes 1368576 | tf_op jit(solution)/shard_map/all_gather | solution.py:13
  76.2 22.3 %copy-start.1 = (s32[64]{0:T(128)S(1)}, s32[64]{0:T(128)}, u32[]{:S(2)}) copy-start(s32[64]{0:T(128)} %param.13) | copy-start | bytes 772
  77.0 17.8 %all-to-all-start.1 = ((bf16[64,8,129]{2,1,0:T(8,128)(2,1)}), bf16[64,8,129]{2,1,0:T(8,128)(2,1)S(1)}, u32[]{:S(2)}, u32[]{:S(2)}) async-start(bf16[64,8,129]{2,1,0:T(8,128)(2,1)} %pad_maximum_fusion), calls=%async_computation.1 | async-start | bytes 524288 | tf_op jit(solution)/shard_map/all_to_all | solution.py:25
  94.7 22.7 %all-to-all-start = ((bf16[64,16,576]{2,1,0:T(8,128)(2,1)}), bf16[64,16,576]{2,1,0:T(8,128)(2,1)S(1)}, u32[]{:S(2)}, u32[]{:S(2)}) async-start(bf16[64,16,576]{2,1,0:T(8,128)(2,1)} %reshape.109), calls=%async_computation | async-start | bytes 2621440 | tf_op jit(solution)/shard_map/all_to_all | solution.py:156
  130.5 5.9 %copy-start = (f32[1024,1024]{0,1:T(8,128)S(1)}, f32[1024,1024]{0,1:T(8,128)}, u32[]{:S(2)}) copy-start(f32[1024,1024]{0,1:T(8,128)} %get-tuple-element.389) | copy-start | bytes 12582916 | tf_op jit(solution)/shard_map/while
  143.9 5.9 %copy-start = (f32[1024,1024]{0,1:T(8,128)S(1)}, f32[1024,1024]{0,1:T(8,128)}, u32[]{:S(2)}) copy-start(f32[1024,1024]{0,1:T(8,128)} %get-tuple-element.389) | copy-start | bytes 12582916 | tf_op jit(solution)/shard_map/while
  157.4 5.9 %copy-start = (f32[1024,1024]{0,1:T(8,128)S(1)}, f32[1024,1024]{0,1:T(8,128)}, u32[]{:S(2)}) copy-start(f32[1024,1024]{0,1:T(8,128)} %get-tuple-element.389) | copy-start | bytes 12582916 | tf_op jit(solution)/shard_map/while
  170.8 5.9 %copy-start = (f32[1024,1024]{0,1:T(8,128)S(1)}, f32[1024,1024]{0,1:T(8,128)}, u32[]{:S(2)}) copy-start(f32[1024,1024]{0,1:T(8,128)} %get-tuple-element.389) | copy-start | bytes 12582916 | tf_op jit(solution)/shard_map/while
Sparse Core Ops, SparseCore 0:
  10.4 63.1 all-gather.2
where the time goes:
time: 232 us; the launch traced here: 231 us
  waiting for transfers between devices  90.1 us (39%)
  blocking collectives  35.4 us (15%)
  other arithmetic  34.3 us (15%)
  matrix products  30.6 us (13%)
  local copies, waits for them, and re-layouts  14.7 us (6%)
  between operations  14.2 us (6%)
  starting transfers between devices  11.5 us (5%)
    all_gather x1, waiting for transfers between devices, side_by_side(): lax.all_gather(both, axis, axis=dim, tiled=True)  63.4 us
    all_to_all x1, blocking collectives, from_everyone(): return lax.all_to_all(copies, axis, split_axis=0, concat_axis=0, tiled=True)  35.4 us
    dot_general x4, matrix products, block_scores(): jnp.einsum('qd,kd->qk', flat_query, cached, preferred_element_type=jnp.fl...  20.1 us
    all_to_all x1, waiting for transfers between devices, body(): lax.all_to_all(gathered[0], 'head', split_axis=0, concat_axis=1, tiled=True)  18.6 us
    reduce_sum x4, other arithmetic, advance(): jnp.sum(jnp.exp(scores - new_max[..., None]), axis=-1)  12.9 us
    dynamic_update_slice x4, other arithmetic, advance(): lax.dynamic_update_slice_in_dim(kept, scores, block_index * block_keys, 2)  9.72 us
    all_to_all x1, waiting for transfers between devices, sent_together(): lax.all_to_all(both, axis, split_axis=split_dim, concat_axis=concat_dim,...  8.07 us
    broadcast_in_dim x1, local copies, waits for them, and re-layouts, first_sweep(): jnp.zeros((row_count, head_count, ctx_keys), jnp.float32)  7.84 us
  transfers between devices with their start and end apart: 3, of which 3 were waited for; matrix products, arithmetic and copies ran while one was open for 1% of the time, Pallas kernels for 0%

commit v1 on v0

v1 whole, which is shorter than its diff:
```python
import functools

import jax
import jax.numpy as jnp
from jax import lax
from jax.experimental import pallas as pl
from jax.experimental.pallas import tpu as pltpu
from jax.sharding import PartitionSpec as P

LOG2E = 1.4426950408889634
ATT = 192.0**-0.5 * LOG2E
HIDDEN = -1e30
BLOCK = 1024
SLOT = 512


def nt(a, b):
    return lax.dot_general(a, b, (((1,), (1,)), ((), ())), preferred_element_type=jnp.float32)


def kernel(
    pack_ref,
    kv_ref,
    ik_ref,
    len_ref,
    target_ref,
    gradient_ref,
    keys,
    rope,
    ikeys,
    queries,
    iqueries,
    iq_flat,
    iw_flat,
    logits,
    p_ref,
    run_max,
    run_sum,
    lse,
    st_own,
    st_core,
    st_core_in,
    st_x,
    st_x_in,
    st_z_in,
    load_sem,
    land_send,
    land_recv,
    step_send,
    last_send,
    side_send,
    side_recv,
    core_s_send,
    core_s_recv,
    x_s_send,
    x_s_recv,
    z_s_send,
    z_s_recv,
):
    c = lax.axis_index("ctx")
    h = lax.axis_index("head")
    x, zl, co = c // 8, (c // 2) % 4, c % 2
    y = h % 4
    n_keys = keys.shape[0]
    nb = n_keys // BLOCK
    nl = BLOCK // 128
    total_keys = n_keys * 32

    def ctx_of(xx, zz):
        return (xx * 4 + zz) * 2 + co

    def device(ctx, head):
        return {"ctx": ctx, "head": head}

    right, left = ctx_of((x + 1) % 4, zl), ctx_of((x + 3) % 4, zl)
    partner = c + 1 - 2 * co

    group = c // 4
    land_x = (x + 2 + y + 4 - group % 4) % 4
    lands = [device(ctx_of(land_x, (zl + k) % 4), group) for k in (2, 1, 3, 0)]
    x_src = h // 2

    def src_y(xx):
        return (xx + 2 + y + 4 - x_src) % 4

    sources = [
        device(ctx_of(x_src, 2 * (h % 2) + zp), zh * 4 + src_y(x)) for zp in (0, 1) for zh in (0, 1)
    ]
    x_others = [device(ctx_of((x + k) % 4, zl), h) for k in (1, 2, 3)]
    z_others = [device(ctx_of(x, (zl + k) % 4), h) for k in (1, 2, 3)]

    load_main = pltpu.make_async_copy(kv_ref.at[:, 0:512], keys.at[:, 0:512], load_sem.at[0])
    load_rope = pltpu.make_async_copy(kv_ref.at[:, 512:576], rope, load_sem.at[1])
    load_ik = pltpu.make_async_copy(ik_ref, ikeys, load_sem.at[2])
    load_rope.start()
    load_ik.start()
    load_main.start()

    barrier = pltpu.get_barrier_semaphore()
    for d in lands + sources + x_others + z_others + [device(partner, h)]:
        pl.semaphore_signal(barrier, inc=1, device_id=d, device_id_type=pl.DeviceIdType.MESH)

    lane = lax.broadcasted_iota(jnp.int32, (1, 128), 1)
    ends = jnp.full((1, 128), 2**30, jnp.int32)
    for r in range(8):
        ends = jnp.where(lane == 64 + r, len_ref[h * 8 + r], ends)
    load_rope.wait()

    def tail(b, carry):
        place = pl.ds(pl.multiple_of(b * 512, 512), 512)
        key = c * n_keys + b * 512 + lax.broadcasted_iota(jnp.int32, (512, 128), 0)
        ext = jnp.where(key < ends, 0.0, HIDDEN).astype(jnp.bfloat16)
        keys[place, 512:640] = jnp.concatenate([rope[place, :], ext[:, 64:]], axis=1)
        return carry

    lax.fori_loop(0, n_keys // 512, tail, 0)

    pl.semaphore_wait(barrier, 15)

    def src_of(kind):
        return pack_ref.at[:, :, 640:768] if kind == 0 else pack_ref.at[:, :, 0:640]

    def place_of(kind, zp, zh, xx):
        buf = iqueries if kind == 0 else queries
        return buf.at[pl.ds(2 * (zp * 2 + co), 2), zh * 4 + src_y(xx)]

    def remote(src, dst, send, recv, d):
        return pltpu.make_async_remote_copy(
            src_ref=src,
            dst_ref=dst,
            send_sem=send,
            recv_sem=recv,
            device_id=d,
            device_id_type=pl.DeviceIdType.MESH,
        )

    sent = []

    def land_copy(kind, k, d):
        buf = iqueries if kind == 0 else queries
        dst = buf.at[pl.ds(2 * (c % 4), 2), h]
        return remote(
            src_of(kind), dst, land_send.at[kind, k], land_recv.at[kind, zl % 2, h // 4, 0], d
        )

    for kind in (0, 1):
        for k, d in enumerate(lands):
            copy = land_copy(kind, k, d)
            copy.start()
            sent.append(copy)

    at_x = [x, (x + 3) % 4, (x + 1) % 4, (x + 2) % 4]

    def arrived(kind, zp, zh, k):
        view = place_of(kind, zp, zh, at_x[k])
        remote(
            view, view, land_send.at[kind, 0], land_recv.at[kind, zp, zh, k], device(right, h)
        ).wait_recv()

    def pass_on(kind, zp):
        for zh in (0, 1):
            arrived(kind, zp, zh, 0)
            view = place_of(kind, zp, zh, x)
            for side, d in enumerate((right, left)):
                copy = remote(
                    view,
                    view,
                    step_send.at[kind, zp, zh, side],
                    land_recv.at[kind, zp, zh, 1 + side],
                    device(d, h),
                )
                copy.start()
                sent.append(copy)

    def pass_last(kind, zp):
        for zh in (0, 1):
            arrived(kind, zp, zh, 1 + zh)
            view = place_of(kind, zp, zh, at_x[1 + zh])
            copy = remote(
                view,
                view,
                last_send.at[kind, zp, zh],
                land_recv.at[kind, zp, zh, 3],
                device((right, left)[zh], h),
            )
            copy.start()
            sent.append(copy)

    def to_partner(kind, zp):
        for zh in (0, 1):
            arrived(kind, zp, zh, 2 - zh)
            arrived(kind, zp, zh, 3)
        buf = iqueries if kind == 0 else queries
        view = buf.at[pl.ds(2 * (zp * 2 + co), 2)]
        copy = remote(
            view, view, side_send.at[kind, zp], side_recv.at[kind, zp], device(partner, h)
        )
        copy.start()
        sent.append(copy)

    def from_partner(kind, zp):
        buf = iqueries if kind == 0 else queries
        view = buf.at[pl.ds(2 * (zp * 2 + 1 - co), 2)]
        remote(
            view, view, side_send.at[kind, zp], side_recv.at[kind, zp], device(partner, h)
        ).wait_recv()

    for zp in (0, 1):
        pass_on(0, zp)
    for zp in (0, 1):
        pass_on(1, zp)
    for zp in (0, 1):
        pass_last(0, zp)
    for zp in (0, 1):
        to_partner(0, zp)
    pass_last(1, 0)
    for zp in (0, 1):
        from_partner(0, zp)

    def combine(parts, scale):
        big = parts[0][0]
        for m, _ in parts[1:]:
            big = jnp.maximum(big, m)
        total = None
        for m, s in parts:
            t = s * jnp.exp2((m - big) * scale)
            total = t if total is None else total + t
        return big, total

    def start_core(e):
        copy = remote(
            st_own.at[e], st_core_in.at[e], core_s_send.at[e], core_s_recv.at[e], device(partner, h)
        )
        copy.start()
        sent.append(copy)

    def start_x(e, scale):
        remote(
            st_own.at[e], st_core_in.at[e], core_s_send.at[e], core_s_recv.at[e], device(partner, h)
        ).wait_recv()
        m, s = combine(
            [(st_own[e, 0], st_own[e, 1]), (st_core_in[e, 0], st_core_in[e, 1])], scale
        )
        st_core[e, 0] = m
        st_core[e, 1] = s
        for k, d in enumerate(x_others):
            copy = remote(
                st_core.at[e], st_x_in.at[e, k], x_s_send.at[e, k], x_s_recv.at[e, k], d
            )
            copy.start()
            sent.append(copy)

    def start_z(e, scale):
        parts = [(st_core[e, 0], st_core[e, 1])]
        for k, d in enumerate(x_others):
            remote(
                st_core.at[e], st_x_in.at[e, k], x_s_send.at[e, k], x_s_recv.at[e, k], d
            ).wait_recv()
            parts.append((st_x_in[e, k, 0], st_x_in[e, k, 1]))
        m, s = combine(parts, scale)
        st_x[e, 0] = m
        st_x[e, 1] = s
        for k, d in enumerate(z_others):
            copy = remote(
                st_x.at[e], st_z_in.at[e, k], z_s_send.at[e, k], z_s_recv.at[e, k], d
            )
            copy.start()
            sent.append(copy)

    def finish(e, scale):
        parts = [(st_x[e, 0], st_x[e, 1])]
        for k, d in enumerate(z_others):
            remote(
                st_x.at[e], st_z_in.at[e, k], z_s_send.at[e, k], z_s_recv.at[e, k], d
            ).wait_recv()
            parts.append((st_z_in[e, k, 0], st_z_in[e, k, 1]))
        return combine(parts, scale)

    for r in range(8):
        both = iqueries[r].astype(jnp.float32)
        iq_flat[r * 64 : (r + 1) * 64, :] = both[:, 0:8, :].reshape(64, 128).astype(jnp.bfloat16)
        iw_flat[r * 64 : (r + 1) * 64, :] = both[:, 8:16, :].reshape(64, 128)
    row = lax.broadcasted_iota(jnp.int32, (8, 1), 0)
    row_ends = jnp.zeros((8, 1), jnp.int32)
    for r in range(8):
        row_ends = jnp.where(row == r, len_ref[h * 8 + r], row_ends)
    load_ik.wait()

    def index_block(b, carry):
        start = pl.multiple_of(b * BLOCK, BLOCK)
        inner = nt(iq_flat[...], ikeys[pl.ds(start, BLOCK), :])
        for i in range(nl):
            lines = []
            for r in range(8):
                acc = None
                for g in range(8):
                    at = r * 64 + g * 8
                    t = jnp.maximum(inner[at : at + 8, i * 128 : (i + 1) * 128], 0.0)
                    t = t * iw_flat[at : at + 8, :]
                    acc = t if acc is None else acc + t
                lines.append(jnp.sum(acc, axis=0, keepdims=True))
            piece = jnp.concatenate(lines, axis=0) * (128.0**-0.5)
            key = c * n_keys + start + i * 128 + lane
            logits[:, pl.ds(start + i * 128, 128)] = jnp.where(key < row_ends, piece, HIDDEN)
        return carry

    lax.fori_loop(0, nb, index_block, 0)
    lg = logits[...]
    idx_max = jnp.max(lg, axis=1, keepdims=True)
    ex_lg = jnp.exp2((lg - idx_max) * LOG2E)
    logits[...] = ex_lg
    st_own[0, 0] = jnp.broadcast_to(idx_max, (8, 128))
    st_own[0, 1] = jnp.broadcast_to(jnp.sum(ex_lg, axis=1, keepdims=True), (8, 128))
    start_core(0)

    to_partner(1, 0)
    pass_last(1, 1)
    load_main.wait()
    from_partner(1, 0)

    def scores(slot, b, before):
        lhs = queries[slot * 4 : slot * 4 + 4].reshape(SLOT, 640)
        s = nt(lhs, keys[b * BLOCK : (b + 1) * BLOCK, :])
        p_ref[slot * SLOT : (slot + 1) * SLOT, b * BLOCK : (b + 1) * BLOCK] = s
        top = s[:, 0:128]
        for i in range(1, nl):
            top = jnp.maximum(top, s[:, i * 128 : (i + 1) * 128])
        run_max[slot * nb + b] = top if b == 0 else jnp.maximum(run_max[slot * nb + b - 1], top)

    def exponentials(slot, b):
        m = run_max[slot * nb + b]
        rows = slice(slot * SLOT, (slot + 1) * SLOT)
        t = None
        for i in range(nl):
            cols = slice(b * BLOCK + i * 128, b * BLOCK + (i + 1) * 128)
            p = jnp.exp2((p_ref[rows, cols] - m) * ATT)
            p_ref[rows, cols] = p
            t = p if t is None else t + p
        if b == 0:
            run_sum[...] = t
        else:
            run_sum[...] = t + run_sum[...] * jnp.exp2((run_max[slot * nb + b - 1] - m) * ATT)

    diagonal = lax.broadcasted_iota(jnp.int32, (128, 128), 0) == lax.broadcasted_iota(
        jnp.int32, (128, 128), 1
    )

    def local_stats(slot):
        m = run_max[slot * nb + nb - 1]
        top = jnp.max(m, axis=1, keepdims=True)
        s = jnp.sum(run_sum[...] * jnp.exp2((m - top) * ATT), axis=1, keepdims=True)
        st_own[1 + slot] = jnp.ones((2, 8, 128), jnp.float32)
        for r in range(4):
            part = slice(r * 128, (r + 1) * 128)
            for plane, value in ((0, top), (1, s)):
                line = jnp.sum(jnp.where(diagonal, value[part], 0.0), axis=0, keepdims=True)
                st_own[1 + slot, plane, r : r + 1, :] = line

    def global_stats(slot):
        m, s = finish(1 + slot, ATT)
        both = m * ATT + jnp.log2(s)
        for r in range(4):
            column = jnp.sum(jnp.where(diagonal, both[r : r + 1, :], 0.0), axis=1, keepdims=True)
            at = slot * SLOT + r * 128
            lse[at : at + 128, :] = jnp.broadcast_to(column, (128, 128))

    gain = 10.0

    def sweep(slot, first, last):
        def block(b, carry):
            start = pl.multiple_of(b * BLOCK, BLOCK)
            for r in range(4):
                acc = [None] * nl
                for k in range(16):
                    at = r * 128 + k * 8
                    g = slot * SLOT + at
                    w = jnp.exp2(
                        run_max[slot * nb + b, at : at + 8, :] * ATT - lse[g : g + 8, :] + gain
                    )
                    for i in range(nl):
                        t = p_ref[g : g + 8, pl.ds(start + i * 128, 128)] * w
                        acc[i] = t if acc[i] is None else acc[i] + t
                for i in range(nl):
                    target_ref[slot * 4 + r : slot * 4 + r + 1, pl.ds(start + i * 128, 128)] = (
                        jnp.sum(acc[i], axis=0, keepdims=True)
                    )
            return carry

        lax.fori_loop(first, last, block, 0)

    scores(0, 0, None)
    start_x(0, LOG2E)
    scores(0, 1, None)
    exponentials(0, 0)
    to_partner(1, 1)
    start_z(0, LOG2E)
    scores(0, 2, None)
    exponentials(0, 1)
    scores(0, 3, None)
    exponentials(0, 2)
    from_partner(1, 1)
    scores(1, 0, None)
    exponentials(0, 3)
    local_stats(0)
    start_core(1)
    scores(1, 1, None)
    exponentials(1, 0)
    start_x(1, ATT)
    scores(1, 2, None)
    exponentials(1, 1)
    start_z(1, ATT)
    scores(1, 3, None)
    exponentials(1, 2)
    exponentials(1, 3)
    local_stats(1)
    start_core(2)
    global_stats(0)
    start_x(2, ATT)
    sweep(0, 0, nb // 2)
    start_z(2, ATT)
    sweep(0, nb // 2, nb)
    m, s = finish(0, LOG2E)
    share = jnp.exp2((st_own[0, 0] - m) * LOG2E) * (total_keys / s)
    share = share[:, 0:1]
    logits[...] = logits[...] * share
    global_stats(1)
    sweep(1, 0, nb)
    gradient_ref[...] = logits[...] - target_ref[...]

    for copy in sent:
        copy.wait_send()


def body(absorbed_query, index_query, index_weight, kv_cache, index_keys, lengths):
    c = lax.axis_index("ctx")
    rows, heads, width = absorbed_query.shape
    n_keys = kv_cache.shape[0]
    slot = 2 * (c % 4) + jnp.arange(rows)
    own = (jnp.arange(64)[None, :] == slot[:, None]).astype(jnp.bfloat16)
    pack = jnp.concatenate(
        [
            absorbed_query,
            jnp.broadcast_to(own[:, None, :], (rows, heads, 64)),
            jnp.concatenate(
                [index_query, jnp.broadcast_to(index_weight[:, :, None], index_query.shape)], axis=1
            ),
        ],
        axis=2,
    )
    dma = pltpu.SemaphoreType.DMA
    f32, bf16 = jnp.float32, jnp.bfloat16
    stats = pltpu.VMEM((3, 2, 8, 128), f32)
    stats3 = pltpu.VMEM((3, 3, 2, 8, 128), f32)
    hbm = pl.BlockSpec(memory_space=pl.ANY)
    return pl.pallas_call(
        kernel,
        out_shape=(
            jax.ShapeDtypeStruct((8, n_keys), f32),
            jax.ShapeDtypeStruct((8, n_keys), f32),
        ),
        in_specs=[hbm, hbm, hbm, pl.BlockSpec(memory_space=pltpu.SMEM)],
        out_specs=(
            pl.BlockSpec(memory_space=pltpu.VMEM),
            pl.BlockSpec(memory_space=pltpu.VMEM),
        ),
        scratch_shapes=[
            pltpu.VMEM((n_keys, 640), bf16),
            pltpu.VMEM((n_keys, 64), bf16),
            pltpu.VMEM((n_keys, 128), bf16),
            pltpu.VMEM((8, 8, 16, 640), bf16),
            pltpu.VMEM((8, 8, 16, 128), bf16),
            pltpu.VMEM((512, 128), bf16),
            pltpu.VMEM((512, 128), f32),
            pltpu.VMEM((8, n_keys), f32),
            pltpu.VMEM((1024, n_keys), f32),
            pltpu.VMEM((2 * (n_keys // BLOCK), SLOT, 128), f32),
            pltpu.VMEM((SLOT, 128), f32),
            pltpu.VMEM((1024, 128), f32),
            stats,
            stats,
            stats,
            stats,
            stats3,
            stats3,
            dma((3,)),
            dma((2, 4)),
            dma((2, 2, 2, 4)),
            dma((2, 2, 2, 2)),
            dma((2, 2, 2)),
            dma((2, 2)),
            dma((2, 2)),
            dma((3,)),
            dma((3,)),
            dma((3, 3)),
            dma((3, 3)),
            dma((3, 3)),
            dma((3, 3)),
        ],
        compiler_params=pltpu.CompilerParams(
            collective_id=0, has_side_effects=True, vmem_limit_bytes=60 * 2**20
        ),
        name="scores_to_gradient",
    )(pack, kv_cache, index_keys, lengths)


def solution(mesh):
    return jax.shard_map(
        body,
        mesh=mesh,
        in_specs=(
            P("ctx", "head", None),
            P("ctx", "head", None),
            P("ctx", "head"),
            P("ctx", None),
            P("ctx", None),
            P(),
        ),
        out_specs=(P("head", "ctx"), P("head", "ctx")),
        check_vma=False,
    )
```

time: 232 us -> 72.4 us (0.31)
  waiting for transfers between devices: 90.1 us -> 0 us
  Pallas kernels: 0 us -> 58.1 us
  blocking collectives: 35.4 us -> 0 us
  other arithmetic: 34.3 us -> 1.57 us
  matrix products: 30.6 us -> 0 us
  between operations: 14.2 us -> 0.66 us
  starting transfers between devices: 11.5 us -> 0 us
  local copies, waits for them, and re-layouts: 14.7 us -> 11.5 us
    all_gather x1 -> x0, waiting for transfers between devices: 63.4 us -> none  [side_by_side(): lax.all_gather(both, axis, axis=dim, tiled=True)]
    pallas_call x0 -> x1, Pallas kernels: none -> 58.1 us  [body(): pl.pallas_call(kernel, out_shape=(jax.ShapeDtypeStruct((8, n_keys), f32),...]
    all_to_all x1 -> x0, blocking collectives: 35.4 us -> none  [from_everyone(): return lax.all_to_all(copies, axis, split_axis=0, concat_axis=0, tiled=True)]
    dot_general x12 -> x0, matrix products: 30.6 us -> none  [the longest x4 20.1 us: block_scores(): jnp.einsum('qd,kd->qk', flat_query, cached, preferred_element_type=jnp.fl...]
    all_to_all x2 -> x0, waiting for transfers between devices: 26.7 us -> none  [the longest x1 18.6 us: body(): lax.all_to_all(gathered[0], 'head', split_axis=0, concat_axis=1, tiled=True)]
    reduce_sum x6 -> x0, other arithmetic: 20.8 us -> none  [the longest x4 12.9 us: advance(): jnp.sum(jnp.exp(scores - new_max[..., None]), axis=-1)]
    all_to_all x2 -> x0, starting transfers between devices: 11.5 us -> none  [the longest x1 7.67 us: sent_together(): lax.all_to_all(both, axis, split_axis=split_dim, concat_axis=concat_dim,...]
    dynamic_update_slice x8 -> x0, other arithmetic: 9.77 us -> none  [the longest x4 9.72 us: advance(): lax.dynamic_update_slice_in_dim(kept, scores, block_index * block_keys, 2)]
  transfers between devices with their start and end apart: 3 -> 0, of which waited for: 3 -> 0; matrix products, arithmetic and copies ran while one was open for 1% -> 0% of each run, Pallas kernels for 0% -> 0%
where the time goes in v1:
time: 72.4 us; the launch traced here: 71.8 us
  Pallas kernels  58.1 us (80%)
  local copies, waits for them, and re-layouts  11.5 us (16%)
  other arithmetic  1.57 us (2%)
    pallas_call x1, Pallas kernels, body(): pl.pallas_call(kernel, out_shape=(jax.ShapeDtypeStruct((8, n_keys), f32),...  58.1 us
    unnamed x3, local copies, waits for them, and re-layouts  10.8 us
    concatenate x1, other arithmetic, body(): jnp.concatenate([absorbed_query, jnp.broadcast_to(own[:, None, :], (rows,...  1.49 us

profile of v1, /device:TPU:1, one launch (start us, length us, event | category | flops | bytes accessed | tf_op | source)
XLA Modules:
  0.0 71.8 jit_solution(839034702334933355)
XLA Ops:
  0.7 0.1 compare_convert_fusion
  0.7 0.7 %broadcast_in_dim.5 = bf16[2,8,128]{2,1,0:T(8,128)(2,1)S(1)} broadcast(bf16[2,8]{1,0:T(2,128)(2,1)} %param.8), dimensions={0,1} | broadcast | bytes 4128 | tf_op jit(solution)/shard_map/broadcast_in_dim | solution.py:445
  1.5 1.5 %maximum_maximum_fusion.pack_ref = bf16[2,16,768]{2,1,0:T(8,128)(2,1)} fusion(bf16[2,8,128]{2,1,0:T(8,128)(2,1)S(1)} %broadcast_in_dim.5, bf16[2,8,128]{2,1,0:T(8,128)(2,1)} %param.7, bf16[2,16,64]{2,1,0:T(8,128)(2,1)S(1)} %broadcast_in_dim.4, bf16[2,16,576]{2,1,0:T(8,128)(2,1)} %param.6), kind=kLoop, calls=%fused_computation | loop fusion | flops 196608 | bytes 98304 | tf_op jit(solution)/shard_map/concatenate | solution.py:440
  3.0 7.7 %copy.8.kv_ref = bf16[4096,576]{1,0:T(8,128)(2,1)} copy(bf16[4096,576]{0,1:T(8,128)(2,1)} %param.9) | data formatting | bytes 9437184 | tf_op args[3]
  10.6 58.1 %scores_to_gradient.1 = (f32[8,4096]{1,0:T(8,128)}, f32[8,4096]{1,0:T(8,128)}) custom-call(bf16[2,16,768]{2,1,0:T(8,128)(2,1)} %maximum_maximum_fusion.pack_ref, bf16[4096,576]{1,0:T(8,128)(2,1)} %copy.8.kv_ref, bf16[4096,128]{1,0:T(8,128)(2,1)} %ik_ref.1, s32[64]{0:T(128)} %len_ref.1), custom_call_target="tpu_custom_call" | custom-call | tf_op jit(solution)/shard_map/scores_to_gradient/pallas_call | solution.py:455
  68.7 1.6 %copy.11 = f32[8,4096]{1,0:T(8,128)} copy(f32[8,4096]{1,0:T(8,128)} %get-tuple-element.4) | data formatting | bytes 262144
  70.3 1.6 %copy.12 = f32[8,4096]{1,0:T(8,128)} copy(f32[8,4096]{1,0:T(8,128)} %get-tuple-element.5) | data formatting | bytes 262144
  (2 shorter events, 0.0 us)

commit v2 on v1

--- a/solution.py
+++ b/solution.py
@@ -19,17 +19,20 @@
 
 
 def kernel(
-    pack_ref,
+    q_ref,
+    iq_ref,
+    iw_ref,
     kv_ref,
     ik_ref,
     len_ref,
-    target_ref,
-    gradient_ref,
+    summed_ref,
+    predicted_ref,
     keys,
-    rope,
     ikeys,
     queries,
+    q_tail,
     iqueries,
+    iweights,
     iq_flat,
     iw_flat,
     logits,
@@ -47,7 +50,6 @@
     land_send,
     land_recv,
     step_send,
-    last_send,
     side_send,
     side_recv,
     core_s_send,
@@ -61,10 +63,9 @@
     h = lax.axis_index("head")
     x, zl, co = c // 8, (c // 2) % 4, c % 2
     y = h % 4
-    n_keys = keys.shape[0]
+    n_keys = keys.shape[1]
     nb = n_keys // BLOCK
     nl = BLOCK // 128
-    total_keys = n_keys * 32
 
     def ctx_of(xx, zz):
         return (xx * 4 + zz) * 2 + co
@@ -72,7 +73,6 @@
     def device(ctx, head):
         return {"ctx": ctx, "head": head}
 
-    right, left = ctx_of((x + 1) % 4, zl), ctx_of((x + 3) % 4, zl)
     partner = c + 1 - 2 * co
 
     group = c // 4
@@ -89,10 +89,8 @@
     x_others = [device(ctx_of((x + k) % 4, zl), h) for k in (1, 2, 3)]
     z_others = [device(ctx_of(x, (zl + k) % 4), h) for k in (1, 2, 3)]
 
-    load_main = pltpu.make_async_copy(kv_ref.at[:, 0:512], keys.at[:, 0:512], load_sem.at[0])
-    load_rope = pltpu.make_async_copy(kv_ref.at[:, 512:576], rope, load_sem.at[1])
-    load_ik = pltpu.make_async_copy(ik_ref, ikeys, load_sem.at[2])
-    load_rope.start()
+    load_main = pltpu.make_async_copy(kv_ref, keys.at[0:576, :], load_sem.at[0])
+    load_ik = pltpu.make_async_copy(ik_ref, ikeys, load_sem.at[1])
     load_ik.start()
     load_main.start()
 
@@ -101,28 +99,27 @@
         pl.semaphore_signal(barrier, inc=1, device_id=d, device_id_type=pl.DeviceIdType.MESH)
 
     lane = lax.broadcasted_iota(jnp.int32, (1, 128), 1)
-    ends = jnp.full((1, 128), 2**30, jnp.int32)
+    row = lax.broadcasted_iota(jnp.int32, (8, 1), 0)
+    row_ends = jnp.zeros((8, 1), jnp.int32)
     for r in range(8):
-        ends = jnp.where(lane == 64 + r, len_ref[h * 8 + r], ends)
-    load_rope.wait()
+        row_ends = jnp.where(row == r, len_ref[h * 8 + r], row_ends)
 
     def tail(b, carry):
-        place = pl.ds(pl.multiple_of(b * 512, 512), 512)
-        key = c * n_keys + b * 512 + lax.broadcasted_iota(jnp.int32, (512, 128), 0)
-        ext = jnp.where(key < ends, 0.0, HIDDEN).astype(jnp.bfloat16)
-        keys[place, 512:640] = jnp.concatenate([rope[place, :], ext[:, 64:]], axis=1)
+        start = pl.multiple_of(b * 512, 512)
+        key = c * n_keys + start + lax.broadcasted_iota(jnp.int32, (8, 512), 1)
+        hide = jnp.where(key < row_ends, 0.0, HIDDEN)
+        lines = jnp.concatenate([hide, jnp.zeros((56, 512), jnp.float32)], axis=0)
+        keys[576:640, pl.ds(start, 512)] = lines.astype(jnp.bfloat16)
         return carry
 
     lax.fori_loop(0, n_keys // 512, tail, 0)
 
     pl.semaphore_wait(barrier, 15)
 
-    def src_of(kind):
-        return pack_ref.at[:, :, 640:768] if kind == 0 else pack_ref.at[:, :, 0:640]
-
-    def place_of(kind, zp, zh, xx):
-        buf = iqueries if kind == 0 else queries
-        return buf.at[pl.ds(2 * (zp * 2 + co), 2), zh * 4 + src_y(xx)]
+    bufs = (iqueries, iweights, queries)
+
+    def rows_of(kind, pair):
+        return pair if kind == 1 else pl.ds(2 * pair, 2)
 
     def remote(src, dst, send, recv, d):
         return pltpu.make_async_remote_copy(
@@ -136,86 +133,79 @@
 
     sent = []
 
-    def land_copy(kind, k, d):
-        buf = iqueries if kind == 0 else queries
-        dst = buf.at[pl.ds(2 * (c % 4), 2), h]
-        return remote(
-            src_of(kind), dst, land_send.at[kind, k], land_recv.at[kind, zl % 2, h // 4, 0], d
-        )
-
-    for kind in (0, 1):
+    def land(kind, start):
         for k, d in enumerate(lands):
-            copy = land_copy(kind, k, d)
-            copy.start()
-            sent.append(copy)
-
-    at_x = [x, (x + 3) % 4, (x + 1) % 4, (x + 2) % 4]
+            copy = remote(
+                (iq_ref, iw_ref, q_ref)[kind],
+                bufs[kind].at[rows_of(kind, c % 4), h],
+                land_send.at[kind, k],
+                land_recv.at[kind, zl % 2, h // 4, 0],
+                d,
+            )
+            if start:
+                copy.start()
+            else:
+                sent.append(copy)
+
+    def view_of(kind, zp, zh, k):
+        return bufs[kind].at[rows_of(kind, zp * 2 + co), zh * 4 + src_y((x + k) % 4)]
 
     def arrived(kind, zp, zh, k):
-        view = place_of(kind, zp, zh, at_x[k])
+        view = view_of(kind, zp, zh, k)
         remote(
-            view, view, land_send.at[kind, 0], land_recv.at[kind, zp, zh, k], device(right, h)
+            view, view, land_send.at[kind, 0], land_recv.at[kind, zp, zh, k], x_others[0]
         ).wait_recv()
 
     def pass_on(kind, zp):
         for zh in (0, 1):
             arrived(kind, zp, zh, 0)
-            view = place_of(kind, zp, zh, x)
-            for side, d in enumerate((right, left)):
+            view = view_of(kind, zp, zh, 0)
+            for step in (2, 1, 3):
                 copy = remote(
                     view,
                     view,
-                    step_send.at[kind, zp, zh, side],
-                    land_recv.at[kind, zp, zh, 1 + side],
-                    device(d, h),
+                    step_send.at[kind, zp, zh, step - 1],
+                    land_recv.at[kind, zp, zh, 4 - step],
+                    x_others[step - 1],
                 )
                 copy.start()
                 sent.append(copy)
 
-    def pass_last(kind, zp):
-        for zh in (0, 1):
-            arrived(kind, zp, zh, 1 + zh)
-            view = place_of(kind, zp, zh, at_x[1 + zh])
-            copy = remote(
-                view,
-                view,
-                last_send.at[kind, zp, zh],
-                land_recv.at[kind, zp, zh, 3],
-                device((right, left)[zh], h),
-            )
-            copy.start()
-            sent.append(copy)
+    def side_copy(kind, zp, core):
+        view = bufs[kind].at[rows_of(kind, zp * 2 + core)]
+        return remote(
+            view, view, side_send.at[kind, zp], side_recv.at[kind, zp], device(partner, h)
+        )
 
     def to_partner(kind, zp):
         for zh in (0, 1):
-            arrived(kind, zp, zh, 2 - zh)
-            arrived(kind, zp, zh, 3)
-        buf = iqueries if kind == 0 else queries
-        view = buf.at[pl.ds(2 * (zp * 2 + co), 2)]
-        copy = remote(
-            view, view, side_send.at[kind, zp], side_recv.at[kind, zp], device(partner, h)
-        )
+            for k in (1, 3, 2):
+                arrived(kind, zp, zh, k)
+        copy = side_copy(kind, zp, co)
         copy.start()
         sent.append(copy)
 
     def from_partner(kind, zp):
-        buf = iqueries if kind == 0 else queries
-        view = buf.at[pl.ds(2 * (zp * 2 + 1 - co), 2)]
-        remote(
-            view, view, side_send.at[kind, zp], side_recv.at[kind, zp], device(partner, h)
-        ).wait_recv()
-
+        side_copy(kind, zp, 1 - co).wait_recv()
+
+    first = zl % 2 == 0
+
+    for kind in (0, 1):
+        land(kind, True)
+    pl.when(first)(lambda: land(2, True))
+    for kind in (0, 1, 2):
+        land(kind, False)
     for zp in (0, 1):
-        pass_on(0, zp)
+        for kind in (0, 1):
+            pass_on(kind, zp)
+    pass_on(2, 0)
+    pl.when(jnp.logical_not(first))(lambda: land(2, True))
     for zp in (0, 1):
-        pass_on(1, zp)
+        for kind in (0, 1):
+            to_partner(kind, zp)
     for zp in (0, 1):
-        pass_last(0, zp)
-    for zp in (0, 1):
-        to_partner(0, zp)
-    pass_last(1, 0)
-    for zp in (0, 1):
-        from_partner(0, zp)
+        for kind in (0, 1):
+            from_partner(kind, zp)
 
     def combine(parts, scale):
         big = parts[0][0]
@@ -276,14 +266,16 @@
             parts.append((st_z_in[e, k, 0], st_z_in[e, k, 1]))
         return combine(parts, scale)
 
+    sub8 = lax.broadcasted_iota(jnp.int32, (8, 8), 0)
+    on_diagonal = sub8 == lax.broadcasted_iota(jnp.int32, (8, 8), 1)
     for r in range(8):
-        both = iqueries[r].astype(jnp.float32)
-        iq_flat[r * 64 : (r + 1) * 64, :] = both[:, 0:8, :].reshape(64, 128).astype(jnp.bfloat16)
-        iw_flat[r * 64 : (r + 1) * 64, :] = both[:, 8:16, :].reshape(64, 128)
-    row = lax.broadcasted_iota(jnp.int32, (8, 1), 0)
-    row_ends = jnp.zeros((8, 1), jnp.int32)
-    for r in range(8):
-        row_ends = jnp.where(row == r, len_ref[h * 8 + r], row_ends)
+        lines = iqueries[r].astype(jnp.float32).reshape(64, 128)
+        iq_flat[r * 64 : (r + 1) * 64, :] = lines.astype(jnp.bfloat16)
+        for g in range(8):
+            w = iweights[r // 2, g].astype(jnp.float32)[r % 2 : r % 2 + 1, :]
+            w = jnp.sum(jnp.where(on_diagonal, w, 0.0), axis=1, keepdims=True)
+            at = r * 64 + g * 8
+            iw_flat[at : at + 8, :] = jnp.broadcast_to(w, (8, 128))
     load_ik.wait()
 
     def index_block(b, carry):
@@ -313,14 +305,23 @@
     st_own[0, 1] = jnp.broadcast_to(jnp.sum(ex_lg, axis=1, keepdims=True), (8, 128))
     start_core(0)
 
-    to_partner(1, 0)
-    pass_last(1, 1)
+    to_partner(2, 0)
+    pass_on(2, 1)
     load_main.wait()
-    from_partner(1, 0)
+    from_partner(2, 0)
 
     def scores(slot, b, before):
-        lhs = queries[slot * 4 : slot * 4 + 4].reshape(SLOT, 640)
-        s = nt(lhs, keys[b * BLOCK : (b + 1) * BLOCK, :])
+        main = queries[slot * 4 : slot * 4 + 4, :, :, 0:512].reshape(SLOT, 512)
+        if b == 0:
+            rotary = queries[slot * 4 : slot * 4 + 4, :, :, 512:576].reshape(SLOT, 64)
+            which = lax.broadcasted_iota(jnp.int32, (SLOT, 64), 0) // 128 + slot * 4
+            own = which == lax.broadcasted_iota(jnp.int32, (SLOT, 64), 1)
+            own = jnp.where(own, 1.0, 0.0).astype(jnp.bfloat16)
+            q_tail[...] = jnp.concatenate([rotary, own], axis=1)
+        lhs = jnp.concatenate([main, q_tail[...]], axis=1)
+        s = jnp.dot(
+            lhs, keys[:, b * BLOCK : (b + 1) * BLOCK], preferred_element_type=jnp.float32
+        )
         p_ref[slot * SLOT : (slot + 1) * SLOT, b * BLOCK : (b + 1) * BLOCK] = s
         top = s[:, 0:128]
         for i in range(1, nl):
@@ -364,7 +365,7 @@
             at = slot * SLOT + r * 128
             lse[at : at + 128, :] = jnp.broadcast_to(column, (128, 128))
 
-    gain = 10.0
+    gain = -7.0
 
     def sweep(slot, first, last):
         def block(b, carry):
@@ -381,7 +382,7 @@
                         t = p_ref[g : g + 8, pl.ds(start + i * 128, 128)] * w
                         acc[i] = t if acc[i] is None else acc[i] + t
                 for i in range(nl):
-                    target_ref[slot * 4 + r : slot * 4 + r + 1, pl.ds(start + i * 128, 128)] = (
+                    summed_ref[slot * 4 + r : slot * 4 + r + 1, pl.ds(start + i * 128, 128)] = (
                         jnp.sum(acc[i], axis=0, keepdims=True)
                     )
             return carry
@@ -392,13 +393,13 @@
     start_x(0, LOG2E)
     scores(0, 1, None)
     exponentials(0, 0)
-    to_partner(1, 1)
+    to_partner(2, 1)
     start_z(0, LOG2E)
     scores(0, 2, None)
     exponentials(0, 1)
     scores(0, 3, None)
     exponentials(0, 2)
-    from_partner(1, 1)
+    from_partner(2, 1)
     scores(1, 0, None)
     exponentials(0, 3)
     local_stats(0)
@@ -420,55 +421,40 @@
     start_z(2, ATT)
     sweep(0, nb // 2, nb)
     m, s = finish(0, LOG2E)
-    share = jnp.exp2((st_own[0, 0] - m) * LOG2E) * (total_keys / s)
-    share = share[:, 0:1]
-    logits[...] = logits[...] * share
+    share = jnp.exp2((st_own[0, 0] - m) * LOG2E) / s
+    predicted_ref[...] = logits[...] * share[:, 0:1]
     global_stats(1)
     sweep(1, 0, nb)
-    gradient_ref[...] = logits[...] - target_ref[...]
 
     for copy in sent:
         copy.wait_send()
 
 
 def body(absorbed_query, index_query, index_weight, kv_cache, index_keys, lengths):
-    c = lax.axis_index("ctx")
-    rows, heads, width = absorbed_query.shape
     n_keys = kv_cache.shape[0]
-    slot = 2 * (c % 4) + jnp.arange(rows)
-    own = (jnp.arange(64)[None, :] == slot[:, None]).astype(jnp.bfloat16)
-    pack = jnp.concatenate(
-        [
-            absorbed_query,
-            jnp.broadcast_to(own[:, None, :], (rows, heads, 64)),
-            jnp.concatenate(
-                [index_query, jnp.broadcast_to(index_weight[:, :, None], index_query.shape)], axis=1
-            ),
-        ],
-        axis=2,
-    )
     dma = pltpu.SemaphoreType.DMA
     f32, bf16 = jnp.float32, jnp.bfloat16
     stats = pltpu.VMEM((3, 2, 8, 128), f32)
     stats3 = pltpu.VMEM((3, 3, 2, 8, 128), f32)
     hbm = pl.BlockSpec(memory_space=pl.ANY)
-    return pl.pallas_call(
+    summed, predicted = pl.pallas_call(
         kernel,
         out_shape=(
             jax.ShapeDtypeStruct((8, n_keys), f32),
             jax.ShapeDtypeStruct((8, n_keys), f32),
         ),
-        in_specs=[hbm, hbm, hbm, pl.BlockSpec(memory_space=pltpu.SMEM)],
+        in_specs=[hbm, hbm, hbm, hbm, hbm, pl.BlockSpec(memory_space=pltpu.SMEM)],
         out_specs=(
             pl.BlockSpec(memory_space=pltpu.VMEM),
             pl.BlockSpec(memory_space=pltpu.VMEM),
         ),
         scratch_shapes=[
-            pltpu.VMEM((n_keys, 640), bf16),
-            pltpu.VMEM((n_keys, 64), bf16),
+            pltpu.VMEM((640, n_keys), bf16),
             pltpu.VMEM((n_keys, 128), bf16),
-            pltpu.VMEM((8, 8, 16, 640), bf16),
-            pltpu.VMEM((8, 8, 16, 128), bf16),
+            pltpu.VMEM((8, 8, 16, 576), bf16),
+            pltpu.VMEM((SLOT, 128), bf16),
+            pltpu.VMEM((8, 8, 8, 128), bf16),
+            pltpu.VMEM((4, 8, 2, 8), bf16),
             pltpu.VMEM((512, 128), bf16),
             pltpu.VMEM((512, 128), f32),
             pltpu.VMEM((8, n_keys), f32),
@@ -482,13 +468,12 @@
             stats,
             stats3,
             stats3,
-            dma((3,)),
-            dma((2, 4)),
-            dma((2, 2, 2, 4)),
-            dma((2, 2, 2, 2)),
-            dma((2, 2, 2)),
-            dma((2, 2)),
-            dma((2, 2)),
+            dma((2,)),
+            dma((3, 4)),
+            dma((3, 2, 2, 4)),
+            dma((3, 2, 2, 3)),
+            dma((3, 2)),
+            dma((3, 2)),
             dma((3,)),
             dma((3,)),
             dma((3, 3)),
@@ -500,7 +485,9 @@
             collective_id=0, has_side_effects=True, vmem_limit_bytes=60 * 2**20
         ),
         name="scores_to_gradient",
-    )(pack, kv_cache, index_keys, lengths)
+    )(absorbed_query, index_query, index_weight, kv_cache.T, index_keys, lengths)
+    keys_total = n_keys * lax.axis_size("ctx")
+    return (keys_total * summed, keys_total * (predicted - summed))
 
 
 def solution(mesh):

time: 72.4 us -> 58.6 us (0.81)
  the two profiles are of different devices: /device:TPU:1 before, /device:TPU:8 now
where the time goes in v2:
time: 58.6 us; the launch traced here: 58.5 us
  Pallas kernels  56.2 us (96%)
  other arithmetic  1.69 us (3%)
  between operations  0.64 us (1%)
    pallas_call x1, Pallas kernels, body(): pl.pallas_call(kernel, out_shape=(jax.ShapeDtypeStruct((8, n_keys), f32),...  56.2 us
    mul x1, other arithmetic, body(): return (keys_total * summed, keys_total * (predicted - summed))  1.69 us

profile of v2, /device:TPU:8, one launch (start us, length us, event | category | flops | bytes accessed | tf_op | source)
XLA Modules:
  0.0 58.5 jit_solution(3424319788800262976)
XLA Ops:
  0.6 56.2 %scores_to_gradient.1 = (f32[8,4096]{1,0:T(8,128)}, f32[8,4096]{1,0:T(8,128)}) custom-call(bf16[2,16,576]{2,1,0:T(8,128)(2,1)} %q_ref.1, bf16[2,8,128]{2,1,0:T(8,128)(2,1)} %iq_ref.1, bf16[2,8]{1,0:T(2,128)(2,1)} %iw_ref.1, bf16[576,4096]{1,0:T(8,128)(2,1)} %bitcast.1, bf16[4096,128]{1,0:T(8,128)(2,1)} %ik_ref.1, s32[64]{0:T(128)} %len_ref.1), custom_call_target="tpu_custom_call" | custom-call | tf_op jit(solution)/shard_map/scores_to_gradient/pallas_call | solution.py:440
  56.8 1.7 %subtract_multiply_fusion = (f32[8,4096]{1,0:T(8,128)}, f32[8,4096]{1,0:T(8,128)}) fusion(f32[8,4096]{1,0:T(8,128)} %get-tuple-element.5, f32[8,4096]{1,0:T(8,128)} %get-tuple-element.4), kind=kLoop, calls=%fused_computation | loop fusion | flops 98304 | bytes 524288 | tf_op jit(solution)/shard_map/mul | solution.py:490

commit v3 on v2

--- a/solution.py
+++ b/solution.py
@@ -41,10 +41,8 @@
     run_sum,
     lse,
     st_own,
-    st_core,
-    st_core_in,
-    st_x,
-    st_x_in,
+    st_near_in,
+    st_near,
     st_z_in,
     load_sem,
     land_send,
@@ -52,10 +50,8 @@
     step_send,
     side_send,
     side_recv,
-    core_s_send,
-    core_s_recv,
-    x_s_send,
-    x_s_recv,
+    near_send,
+    near_recv,
     z_s_send,
     z_s_recv,
 ):
@@ -87,6 +83,7 @@
         device(ctx_of(x_src, 2 * (h % 2) + zp), zh * 4 + src_y(x)) for zp in (0, 1) for zh in (0, 1)
     ]
     x_others = [device(ctx_of((x + k) % 4, zl), h) for k in (1, 2, 3)]
+    near = [device(((x + k // 2) % 4 * 4 + zl) * 2 + (co + k) % 2, h) for k in range(1, 8)]
     z_others = [device(ctx_of(x, (zl + k) % 4), h) for k in (1, 2, 3)]
 
     load_main = pltpu.make_async_copy(kv_ref, keys.at[0:576, :], load_sem.at[0])
@@ -95,7 +92,7 @@
     load_main.start()
 
     barrier = pltpu.get_barrier_semaphore()
-    for d in lands + sources + x_others + z_others + [device(partner, h)]:
+    for d in lands + sources + near + z_others:
         pl.semaphore_signal(barrier, inc=1, device_id=d, device_id_type=pl.DeviceIdType.MESH)
 
     lane = lax.broadcasted_iota(jnp.int32, (1, 128), 1)
@@ -114,7 +111,7 @@
 
     lax.fori_loop(0, n_keys // 512, tail, 0)
 
-    pl.semaphore_wait(barrier, 15)
+    pl.semaphore_wait(barrier, 18)
 
     bufs = (iqueries, iweights, queries)
 
@@ -190,22 +187,18 @@
 
     first = zl % 2 == 0
 
+    pl.when(first)(lambda: land(2, True))
     for kind in (0, 1):
         land(kind, True)
-    pl.when(first)(lambda: land(2, True))
     for kind in (0, 1, 2):
         land(kind, False)
-    for zp in (0, 1):
-        for kind in (0, 1):
-            pass_on(kind, zp)
     pass_on(2, 0)
     pl.when(jnp.logical_not(first))(lambda: land(2, True))
     for zp in (0, 1):
         for kind in (0, 1):
-            to_partner(kind, zp)
-    for zp in (0, 1):
-        for kind in (0, 1):
-            from_partner(kind, zp)
+            pass_on(kind, zp)
+    to_partner(2, 0)
+    load_main.wait()
 
     def combine(parts, scale):
         big = parts[0][0]
@@ -217,66 +210,65 @@
             total = t if total is None else total + t
         return big, total
 
-    def start_core(e):
-        copy = remote(
-            st_own.at[e], st_core_in.at[e], core_s_send.at[e], core_s_recv.at[e], device(partner, h)
+    def near_copy(e, k):
+        back = (4 - k // 2) % 4 * 2 + k % 2
+        return remote(
+            st_own.at[e],
+            st_near_in.at[e, back - 1],
+            near_send.at[e, k - 1],
+            near_recv.at[e, back - 1],
+            near[k - 1],
         )
-        copy.start()
-        sent.append(copy)
-
-    def start_x(e, scale):
-        remote(
-            st_own.at[e], st_core_in.at[e], core_s_send.at[e], core_s_recv.at[e], device(partner, h)
-        ).wait_recv()
-        m, s = combine(
-            [(st_own[e, 0], st_own[e, 1]), (st_core_in[e, 0], st_core_in[e, 1])], scale
-        )
-        st_core[e, 0] = m
-        st_core[e, 1] = s
-        for k, d in enumerate(x_others):
-            copy = remote(
-                st_core.at[e], st_x_in.at[e, k], x_s_send.at[e, k], x_s_recv.at[e, k], d
-            )
+
+    def start_near(e):
+        for k in (4, 5, 2, 3, 6, 7, 1):
+            copy = near_copy(e, k)
             copy.start()
             sent.append(copy)
 
     def start_z(e, scale):
-        parts = [(st_core[e, 0], st_core[e, 1])]
-        for k, d in enumerate(x_others):
-            remote(
-                st_core.at[e], st_x_in.at[e, k], x_s_send.at[e, k], x_s_recv.at[e, k], d
-            ).wait_recv()
-            parts.append((st_x_in[e, k, 0], st_x_in[e, k, 1]))
+        parts = [(st_own[e, 0], st_own[e, 1])]
+        for k in range(1, 8):
+            near_copy(e, k).wait_recv()
+        for k in range(1, 8):
+            parts.append((st_near_in[e, k - 1, 0], st_near_in[e, k - 1, 1]))
         m, s = combine(parts, scale)
-        st_x[e, 0] = m
-        st_x[e, 1] = s
-        for k, d in enumerate(z_others):
-            copy = remote(
-                st_x.at[e], st_z_in.at[e, k], z_s_send.at[e, k], z_s_recv.at[e, k], d
-            )
+        st_near[e, 0] = m
+        st_near[e, 1] = s
+        for k in (1, 3, 2):
+            copy = z_copy(e, k)
             copy.start()
             sent.append(copy)
 
+    def z_copy(e, k):
+        return remote(
+            st_near.at[e],
+            st_z_in.at[e, 3 - k],
+            z_s_send.at[e, k - 1],
+            z_s_recv.at[e, 3 - k],
+            z_others[k - 1],
+        )
+
     def finish(e, scale):
-        parts = [(st_x[e, 0], st_x[e, 1])]
-        for k, d in enumerate(z_others):
-            remote(
-                st_x.at[e], st_z_in.at[e, k], z_s_send.at[e, k], z_s_recv.at[e, k], d
-            ).wait_recv()
-            parts.append((st_z_in[e, k, 0], st_z_in[e, k, 1]))
+        parts = [(st_near[e, 0], st_near[e, 1])]
+        for k in (1, 2, 3):
+            z_copy(e, k).wait_recv()
+        for k in (1, 2, 3):
+            parts.append((st_z_in[e, k - 1, 0], st_z_in[e, k - 1, 1]))
         return combine(parts, scale)
 
     sub8 = lax.broadcasted_iota(jnp.int32, (8, 8), 0)
     on_diagonal = sub8 == lax.broadcasted_iota(jnp.int32, (8, 8), 1)
-    for r in range(8):
-        lines = iqueries[r].astype(jnp.float32).reshape(64, 128)
-        iq_flat[r * 64 : (r + 1) * 64, :] = lines.astype(jnp.bfloat16)
-        for g in range(8):
-            w = iweights[r // 2, g].astype(jnp.float32)[r % 2 : r % 2 + 1, :]
-            w = jnp.sum(jnp.where(on_diagonal, w, 0.0), axis=1, keepdims=True)
-            at = r * 64 + g * 8
-            iw_flat[at : at + 8, :] = jnp.broadcast_to(w, (8, 128))
-    load_ik.wait()
+
+    def index_queries():
+        for r in range(8):
+            lines = iqueries[r].astype(jnp.float32).reshape(64, 128)
+            iq_flat[r * 64 : (r + 1) * 64, :] = lines.astype(jnp.bfloat16)
+            for g in range(8):
+                w = iweights[r // 2, g].astype(jnp.float32)[r % 2 : r % 2 + 1, :]
+                w = jnp.sum(jnp.where(on_diagonal, w, 0.0), axis=1, keepdims=True)
+                at = r * 64 + g * 8
+                iw_flat[at : at + 8, :] = jnp.broadcast_to(w, (8, 128))
 
     def index_block(b, carry):
         start = pl.multiple_of(b * BLOCK, BLOCK)
@@ -296,21 +288,15 @@
             logits[:, pl.ds(start + i * 128, 128)] = jnp.where(key < row_ends, piece, HIDDEN)
         return carry
 
-    lax.fori_loop(0, nb, index_block, 0)
-    lg = logits[...]
-    idx_max = jnp.max(lg, axis=1, keepdims=True)
-    ex_lg = jnp.exp2((lg - idx_max) * LOG2E)
-    logits[...] = ex_lg
-    st_own[0, 0] = jnp.broadcast_to(idx_max, (8, 128))
-    st_own[0, 1] = jnp.broadcast_to(jnp.sum(ex_lg, axis=1, keepdims=True), (8, 128))
-    start_core(0)
-
-    to_partner(2, 0)
-    pass_on(2, 1)
-    load_main.wait()
-    from_partner(2, 0)
-
-    def scores(slot, b, before):
+    def index_stats():
+        lg = logits[...]
+        idx_max = jnp.max(lg, axis=1, keepdims=True)
+        ex_lg = jnp.exp2((lg - idx_max) * LOG2E)
+        logits[...] = ex_lg
+        st_own[0, 0] = jnp.broadcast_to(idx_max, (8, 128))
+        st_own[0, 1] = jnp.broadcast_to(jnp.sum(ex_lg, axis=1, keepdims=True), (8, 128))
+
+    def scores(slot, b):
         main = queries[slot * 4 : slot * 4 + 4, :, :, 0:512].reshape(SLOT, 512)
         if b == 0:
             rotary = queries[slot * 4 : slot * 4 + 4, :, :, 512:576].reshape(SLOT, 64)
@@ -389,40 +375,54 @@
 
         lax.fori_loop(first, last, block, 0)
 
-    scores(0, 0, None)
-    start_x(0, LOG2E)
-    scores(0, 1, None)
+    from_partner(2, 0)
+    scores(0, 0)
+    pass_on(2, 1)
+    scores(0, 1)
     exponentials(0, 0)
-    to_partner(2, 1)
-    start_z(0, LOG2E)
-    scores(0, 2, None)
+    for zp in (0, 1):
+        for kind in (0, 1):
+            to_partner(kind, zp)
+    scores(0, 2)
     exponentials(0, 1)
-    scores(0, 3, None)
+    for zp in (0, 1):
+        for kind in (0, 1):
+            from_partner(kind, zp)
+    load_ik.wait()
+    scores(0, 3)
     exponentials(0, 2)
-    from_partner(2, 1)
-    scores(1, 0, None)
+    index_queries()
     exponentials(0, 3)
     local_stats(0)
-    start_core(1)
-    scores(1, 1, None)
+    start_near(1)
+    lax.fori_loop(0, nb // 2, index_block, 0)
+    to_partner(2, 1)
+    lax.fori_loop(nb // 2, nb, index_block, 0)
+    index_stats()
+    start_near(0)
+    from_partner(2, 1)
+    scores(1, 0)
+    start_z(1, ATT)
+    scores(1, 1)
     exponentials(1, 0)
-    start_x(1, ATT)
-    scores(1, 2, None)
+    scores(1, 2)
     exponentials(1, 1)
-    start_z(1, ATT)
-    scores(1, 3, None)
+    start_z(0, LOG2E)
+    scores(1, 3)
     exponentials(1, 2)
     exponentials(1, 3)
     local_stats(1)
-    start_core(2)
+    earlier = list(sent)
+    sent.clear()
+    start_near(2)
     global_stats(0)
-    start_x(2, ATT)
-    sweep(0, 0, nb // 2)
-    start_z(2, ATT)
-    sweep(0, nb // 2, nb)
+    sweep(0, 0, nb)
+    for copy in earlier:
+        copy.wait_send()
     m, s = finish(0, LOG2E)
     share = jnp.exp2((st_own[0, 0] - m) * LOG2E) / s
     predicted_ref[...] = logits[...] * share[:, 0:1]
+    start_z(2, ATT)
     global_stats(1)
     sweep(1, 0, nb)
 
@@ -434,16 +434,19 @@
     n_keys = kv_cache.shape[0]
     dma = pltpu.SemaphoreType.DMA
     f32, bf16 = jnp.float32, jnp.bfloat16
-    stats = pltpu.VMEM((3, 2, 8, 128), f32)
-    stats3 = pltpu.VMEM((3, 3, 2, 8, 128), f32)
-    hbm = pl.BlockSpec(memory_space=pl.ANY)
+    stats = [pltpu.VMEM((3, *n, 2, 8, 128), f32) for n in ((), (7,), (), (3,))]
+    hbm = pl.BlockSpec(memory_space=pltpu.HBM)
+    in_hbm = [
+        pltpu.with_memory_space_constraint(a, pltpu.HBM)
+        for a in (absorbed_query, index_query, index_weight, kv_cache.T, index_keys, lengths)
+    ]
     summed, predicted = pl.pallas_call(
         kernel,
         out_shape=(
             jax.ShapeDtypeStruct((8, n_keys), f32),
             jax.ShapeDtypeStruct((8, n_keys), f32),
         ),
-        in_specs=[hbm, hbm, hbm, hbm, hbm, pl.BlockSpec(memory_space=pltpu.SMEM)],
+        in_specs=[hbm] * 5 + [pl.BlockSpec(memory_space=pltpu.SMEM)],
         out_specs=(
             pl.BlockSpec(memory_space=pltpu.VMEM),
             pl.BlockSpec(memory_space=pltpu.VMEM),
@@ -462,30 +465,23 @@
             pltpu.VMEM((2 * (n_keys // BLOCK), SLOT, 128), f32),
             pltpu.VMEM((SLOT, 128), f32),
             pltpu.VMEM((1024, 128), f32),
-            stats,
-            stats,
-            stats,
-            stats,
-            stats3,
-            stats3,
+            *stats,
             dma((2,)),
             dma((3, 4)),
             dma((3, 2, 2, 4)),
             dma((3, 2, 2, 3)),
             dma((3, 2)),
             dma((3, 2)),
-            dma((3,)),
-            dma((3,)),
-            dma((3, 3)),
-            dma((3, 3)),
+            dma((3, 7)),
+            dma((3, 7)),
             dma((3, 3)),
             dma((3, 3)),
         ],
         compiler_params=pltpu.CompilerParams(
-            collective_id=0, has_side_effects=True, vmem_limit_bytes=60 * 2**20
+            collective_id=0, has_side_effects=True, vmem_limit_bytes=36 * 2**20
         ),
         name="scores_to_gradient",
-    )(absorbed_query, index_query, index_weight, kv_cache.T, index_keys, lengths)
+    )(*in_hbm)
     keys_total = n_keys * lax.axis_size("ctx")
     return (keys_total * summed, keys_total * (predicted - summed))
 

time: 58.6 us -> 52.2 us (0.89)
  the two profiles are of different devices: /device:TPU:8 before, /device:TPU:1 now
where the time goes in v3:
time: 52.2 us; the launch traced here: 52.1 us
  Pallas kernels  50.7 us (97%)
  other arithmetic  0.72 us (1%)
  between operations  0.64 us (1%)
    pallas_call x1, Pallas kernels, body(): pl.pallas_call(kernel, out_shape=(jax.ShapeDtypeStruct((8, n_keys), f32),...  50.7 us

profile of v3, /device:TPU:1, one launch (start us, length us, event | category | flops | bytes accessed | tf_op | source)
XLA Modules:
  0.0 52.1 jit_solution(5050819190514518867)
XLA Ops:
  0.6 50.7 %scores_to_gradient.1 = (f32[8,4096]{1,0:T(8,128)S(1)}, f32[8,4096]{1,0:T(8,128)S(1)}) custom-call(bf16[2,16,576]{2,1,0:T(8,128)(2,1)} %q_ref.1, bf16[2,8,128]{2,1,0:T(8,128)(2,1)} %iq_ref.1, bf16[2,8]{1,0:T(2,128)(2,1)} %iw_ref.1, bf16[576,4096]{1,0:T(8,128)(2,1)} %bitcast.1, bf16[4096,128]{1,0:T(8,128)(2,1)} %ik_ref.1, s32[64]{0:T(128)} %len_ref.1), custom_call_target="tpu_custom_call" | custom-call | tf_op jit(solution)/shard_map/scores_to_gradient/pallas_call | solution.py:443
  51.4 0.7 %subtract_multiply_fusion = (f32[8,4096]{1,0:T(8,128)}, f32[8,4096]{1,0:T(8,128)}) fusion(f32[8,4096]{1,0:T(8,128)S(1)} %get-tuple-element.5, f32[8,4096]{1,0:T(8,128)S(1)} %get-tuple-element.4), kind=kLoop, calls=%fused_computation | loop fusion | flops 98304 | bytes 524288 | tf_op jit(solution)/shard_map/mul | solution.py:486

commit v4 on v3

--- a/solution.py
+++ b/solution.py
@@ -12,6 +12,8 @@
 HIDDEN = -1e30
 BLOCK = 1024
 SLOT = 512
+PIECES = 1
+ORDER = ("old", "new")
 
 
 def nt(a, b):
@@ -30,7 +32,7 @@
     keys,
     ikeys,
     queries,
-    q_tail,
+    q_slot,
     iqueries,
     iweights,
     iq_flat,
@@ -154,14 +156,15 @@
         ).wait_recv()
 
     def pass_on(kind, zp):
-        for zh in (0, 1):
+        for i in (0, 1):
+            zh = (h // 4 + i) % 2
             arrived(kind, zp, zh, 0)
             view = view_of(kind, zp, zh, 0)
             for step in (2, 1, 3):
                 copy = remote(
                     view,
                     view,
-                    step_send.at[kind, zp, zh, step - 1],
+                    step_send.at[kind, zp, i, step - 1],
                     land_recv.at[kind, zp, zh, 4 - step],
                     x_others[step - 1],
                 )
@@ -296,37 +299,56 @@
         st_own[0, 0] = jnp.broadcast_to(idx_max, (8, 128))
         st_own[0, 1] = jnp.broadcast_to(jnp.sum(ex_lg, axis=1, keepdims=True), (8, 128))
 
-    def scores(slot, b):
-        main = queries[slot * 4 : slot * 4 + 4, :, :, 0:512].reshape(SLOT, 512)
-        if b == 0:
-            rotary = queries[slot * 4 : slot * 4 + 4, :, :, 512:576].reshape(SLOT, 64)
-            which = lax.broadcasted_iota(jnp.int32, (SLOT, 64), 0) // 128 + slot * 4
-            own = which == lax.broadcasted_iota(jnp.int32, (SLOT, 64), 1)
-            own = jnp.where(own, 1.0, 0.0).astype(jnp.bfloat16)
-            q_tail[...] = jnp.concatenate([rotary, own], axis=1)
-        lhs = jnp.concatenate([main, q_tail[...]], axis=1)
-        s = jnp.dot(
-            lhs, keys[:, b * BLOCK : (b + 1) * BLOCK], preferred_element_type=jnp.float32
-        )
-        p_ref[slot * SLOT : (slot + 1) * SLOT, b * BLOCK : (b + 1) * BLOCK] = s
-        top = s[:, 0:128]
-        for i in range(1, nl):
-            top = jnp.maximum(top, s[:, i * 128 : (i + 1) * 128])
-        run_max[slot * nb + b] = top if b == 0 else jnp.maximum(run_max[slot * nb + b - 1], top)
-
-    def exponentials(slot, b):
-        m = run_max[slot * nb + b]
-        rows = slice(slot * SLOT, (slot + 1) * SLOT)
-        t = None
-        for i in range(nl):
-            cols = slice(b * BLOCK + i * 128, b * BLOCK + (i + 1) * 128)
-            p = jnp.exp2((p_ref[rows, cols] - m) * ATT)
-            p_ref[rows, cols] = p
-            t = p if t is None else t + p
-        if b == 0:
-            run_sum[...] = t
-        else:
-            run_sum[...] = t + run_sum[...] * jnp.exp2((run_max[slot * nb + b - 1] - m) * ATT)
+    def take_queries(slot):
+        rows = slice(slot * 4, slot * 4 + 4)
+        q_slot[:, 0:512] = queries[rows, :, :, 0:512].reshape(SLOT, 512)
+        rotary = queries[rows, :, :, 512:576].reshape(SLOT, 64)
+        which = lax.broadcasted_iota(jnp.int32, (SLOT, 64), 0) // 128 + slot * 4
+        own = which == lax.broadcasted_iota(jnp.int32, (SLOT, 64), 1)
+        own = jnp.where(own, 1.0, 0.0).astype(jnp.bfloat16)
+        q_slot[:, 512:640] = jnp.concatenate([rotary, own], axis=1)
+
+    def step(new, old):
+        width = BLOCK // PIECES
+        top = total = None
+        if new is not None and new[1] == 0:
+            take_queries(new[0])
+        for j in range(PIECES):
+            for side in ORDER:
+                if side == "old" and old is not None:
+                    slot, b = old
+                    rows = slice(slot * SLOT, (slot + 1) * SLOT)
+                    m = run_max[slot * nb + b]
+                    for i in range(width // 128):
+                        at = b * BLOCK + j * width + i * 128
+                        p = jnp.exp2((p_ref[rows, at : at + 128] - m) * ATT)
+                        p_ref[rows, at : at + 128] = p
+                        total = p if total is None else total + p
+                if side == "new" and new is not None:
+                    slot, b = new
+                    rows = slice(slot * SLOT, (slot + 1) * SLOT)
+                    at = b * BLOCK + j * width
+                    s = jnp.dot(
+                        q_slot[...], keys[:, at : at + width], preferred_element_type=jnp.float32
+                    )
+                    p_ref[rows, at : at + width] = s
+                    for i in range(width // 128):
+                        part = s[:, i * 128 : (i + 1) * 128]
+                        top = part if top is None else jnp.maximum(top, part)
+        if old is not None:
+            slot, b = old
+            if b == 0:
+                run_sum[...] = total
+            else:
+                m = run_max[slot * nb + b]
+                run_sum[...] = total + run_sum[...] * jnp.exp2(
+                    (run_max[slot * nb + b - 1] - m) * ATT
+                )
+        if new is not None:
+            slot, b = new
+            if b > 0:
+                top = jnp.maximum(run_max[slot * nb + b - 1], top)
+            run_max[slot * nb + b] = top
 
     diagonal = lax.broadcasted_iota(jnp.int32, (128, 128), 0) == lax.broadcasted_iota(
         jnp.int32, (128, 128), 1
@@ -376,53 +398,47 @@
         lax.fori_loop(first, last, block, 0)
 
     from_partner(2, 0)
-    scores(0, 0)
+    step((0, 0), None)
     pass_on(2, 1)
-    scores(0, 1)
-    exponentials(0, 0)
     for zp in (0, 1):
         for kind in (0, 1):
             to_partner(kind, zp)
-    scores(0, 2)
-    exponentials(0, 1)
+    step((0, 1), (0, 0))
+    step((0, 2), (0, 1))
+    step((0, 3), (0, 2))
+    step(None, (0, 3))
+    local_stats(0)
+    start_near(1)
     for zp in (0, 1):
         for kind in (0, 1):
             from_partner(kind, zp)
     load_ik.wait()
-    scores(0, 3)
-    exponentials(0, 2)
     index_queries()
-    exponentials(0, 3)
-    local_stats(0)
-    start_near(1)
     lax.fori_loop(0, nb // 2, index_block, 0)
     to_partner(2, 1)
     lax.fori_loop(nb // 2, nb, index_block, 0)
     index_stats()
     start_near(0)
     from_partner(2, 1)
-    scores(1, 0)
+    step((1, 0), None)
     start_z(1, ATT)
-    scores(1, 1)
-    exponentials(1, 0)
-    scores(1, 2)
-    exponentials(1, 1)
-    start_z(0, LOG2E)
-    scores(1, 3)
-    exponentials(1, 2)
-    exponentials(1, 3)
+    step((1, 1), (1, 0))
+    step((1, 2), (1, 1))
+    step((1, 3), (1, 2))
+    step(None, (1, 3))
     local_stats(1)
     earlier = list(sent)
     sent.clear()
     start_near(2)
+    start_z(0, LOG2E)
     global_stats(0)
     sweep(0, 0, nb)
     for copy in earlier:
         copy.wait_send()
+    start_z(2, ATT)
     m, s = finish(0, LOG2E)
     share = jnp.exp2((st_own[0, 0] - m) * LOG2E) / s
     predicted_ref[...] = logits[...] * share[:, 0:1]
-    start_z(2, ATT)
     global_stats(1)
     sweep(1, 0, nb)
 
@@ -455,7 +471,7 @@
             pltpu.VMEM((640, n_keys), bf16),
             pltpu.VMEM((n_keys, 128), bf16),
             pltpu.VMEM((8, 8, 16, 576), bf16),
-            pltpu.VMEM((SLOT, 128), bf16),
+            pltpu.VMEM((SLOT, 640), bf16),
             pltpu.VMEM((8, 8, 8, 128), bf16),
             pltpu.VMEM((4, 8, 2, 8), bf16),
             pltpu.VMEM((512, 128), bf16),

time: 52.2 us -> 51 us (0.977)
  Pallas kernels: 50.7 us -> 49.6 us
    pallas_call x1, Pallas kernels: 50.7 us -> 49.6 us  [body(): pl.pallas_call(kernel, out_shape=(jax.ShapeDtypeStruct((8, n_keys), f32),...]
where the time goes in v4:
time: 51 us; the launch traced here: 50.9 us
  Pallas kernels  49.6 us (97%)
  other arithmetic  0.72 us (1%)
  between operations  0.64 us (1%)
    pallas_call x1, Pallas kernels, body(): pl.pallas_call(kernel, out_shape=(jax.ShapeDtypeStruct((8, n_keys), f32),...  49.6 us

profile of v4, /device:TPU:1, one launch (start us, length us, event | category | flops | bytes accessed | tf_op | source)
XLA Modules:
  0.0 50.9 jit_solution(2871535997264497382)
XLA Ops:
  0.6 49.6 %scores_to_gradient.1 = (f32[8,4096]{1,0:T(8,128)S(1)}, f32[8,4096]{1,0:T(8,128)S(1)}) custom-call(bf16[2,16,576]{2,1,0:T(8,128)(2,1)} %q_ref.1, bf16[2,8,128]{2,1,0:T(8,128)(2,1)} %iq_ref.1, bf16[2,8]{1,0:T(2,128)(2,1)} %iw_ref.1, bf16[576,4096]{1,0:T(8,128)(2,1)} %bitcast.1, bf16[4096,128]{1,0:T(8,128)(2,1)} %ik_ref.1, s32[64]{0:T(128)} %len_ref.1), custom_call_target="tpu_custom_call" | custom-call | tf_op jit(solution)/shard_map/scores_to_gradient/pallas_call | solution.py:459
  50.2 0.7 %subtract_multiply_fusion = (f32[8,4096]{1,0:T(8,128)}, f32[8,4096]{1,0:T(8,128)}) fusion(f32[8,4096]{1,0:T(8,128)S(1)} %get-tuple-element.5, f32[8,4096]{1,0:T(8,128)S(1)} %get-tuple-element.4), kind=kLoop, calls=%fused_computation | loop fusion | flops 98304 | bytes 524288 | tf_op jit(solution)/shard_map/mul | solution.py:502

commit v5 on v4

--- a/solution.py
+++ b/solution.py
@@ -12,8 +12,6 @@
 HIDDEN = -1e30
 BLOCK = 1024
 SLOT = 512
-PIECES = 1
-ORDER = ("old", "new")
 
 
 def nt(a, b):
@@ -299,56 +297,58 @@
         st_own[0, 0] = jnp.broadcast_to(idx_max, (8, 128))
         st_own[0, 1] = jnp.broadcast_to(jnp.sum(ex_lg, axis=1, keepdims=True), (8, 128))
 
-    def take_queries(slot):
-        rows = slice(slot * 4, slot * 4 + 4)
-        q_slot[:, 0:512] = queries[rows, :, :, 0:512].reshape(SLOT, 512)
-        rotary = queries[rows, :, :, 512:576].reshape(SLOT, 64)
-        which = lax.broadcasted_iota(jnp.int32, (SLOT, 64), 0) // 128 + slot * 4
-        own = which == lax.broadcasted_iota(jnp.int32, (SLOT, 64), 1)
+    def place(slot, half):
+        if half is None:
+            return pl.ds(0, SLOT), pl.ds(slot * SLOT, SLOT)
+        size = SLOT // 2
+        start = pl.multiple_of(half * size, size)
+        return pl.ds(start, size), pl.ds(pl.multiple_of(slot * SLOT + start, size), size)
+
+    def take_queries(slot, half):
+        local, _ = place(slot, half)
+        n = SLOT if half is None else SLOT // 2
+        rows = pl.ds(slot * 4, 4) if half is None else pl.ds(slot * 4 + half * 2, 2)
+        first_row = slot * 4 if half is None else slot * 4 + half * 2
+        q_slot[local, 0:512] = queries[rows, :, :, 0:512].reshape(n, 512)
+        rotary = queries[rows, :, :, 512:576].reshape(n, 64)
+        which = lax.broadcasted_iota(jnp.int32, (n, 64), 0) // 128 + first_row
+        own = which == lax.broadcasted_iota(jnp.int32, (n, 64), 1)
         own = jnp.where(own, 1.0, 0.0).astype(jnp.bfloat16)
-        q_slot[:, 512:640] = jnp.concatenate([rotary, own], axis=1)
+        q_slot[local, 512:640] = jnp.concatenate([rotary, own], axis=1)
 
     def step(new, old):
-        width = BLOCK // PIECES
-        top = total = None
-        if new is not None and new[1] == 0:
-            take_queries(new[0])
-        for j in range(PIECES):
-            for side in ORDER:
-                if side == "old" and old is not None:
-                    slot, b = old
-                    rows = slice(slot * SLOT, (slot + 1) * SLOT)
-                    m = run_max[slot * nb + b]
-                    for i in range(width // 128):
-                        at = b * BLOCK + j * width + i * 128
-                        p = jnp.exp2((p_ref[rows, at : at + 128] - m) * ATT)
-                        p_ref[rows, at : at + 128] = p
-                        total = p if total is None else total + p
-                if side == "new" and new is not None:
-                    slot, b = new
-                    rows = slice(slot * SLOT, (slot + 1) * SLOT)
-                    at = b * BLOCK + j * width
-                    s = jnp.dot(
-                        q_slot[...], keys[:, at : at + width], preferred_element_type=jnp.float32
-                    )
-                    p_ref[rows, at : at + width] = s
-                    for i in range(width // 128):
-                        part = s[:, i * 128 : (i + 1) * 128]
-                        top = part if top is None else jnp.maximum(top, part)
+        if new is not None:
+            slot, b, half = new
+            if b == 0:
+                take_queries(slot, half)
+            local, rows = place(slot, half)
+            at = b * BLOCK
+            s = jnp.dot(
+                q_slot[local, :], keys[:, at : at + BLOCK], preferred_element_type=jnp.float32
+            )
+            p_ref[rows, at : at + BLOCK] = s
+            top = s[:, 0:128]
+            for i in range(1, nl):
+                top = jnp.maximum(top, s[:, i * 128 : (i + 1) * 128])
+            if b > 0:
+                top = jnp.maximum(run_max[slot * nb + b - 1, local, :], top)
         if old is not None:
-            slot, b = old
-            if b == 0:
-                run_sum[...] = total
-            else:
-                m = run_max[slot * nb + b]
-                run_sum[...] = total + run_sum[...] * jnp.exp2(
-                    (run_max[slot * nb + b - 1] - m) * ATT
-                )
+            slot, b, half = old
+            local, rows = place(slot, half)
+            m = run_max[slot * nb + b, local, :]
+            total = None
+            for i in range(nl):
+                at = b * BLOCK + i * 128
+                p = jnp.exp2((p_ref[rows, at : at + 128] - m) * ATT)
+                p_ref[rows, at : at + 128] = p
+                total = p if total is None else total + p
+            if b > 0:
+                scale = jnp.exp2((run_max[slot * nb + b - 1, local, :] - m) * ATT)
+                total = total + run_sum[local, :] * scale
+            run_sum[local, :] = total
         if new is not None:
-            slot, b = new
-            if b > 0:
-                top = jnp.maximum(run_max[slot * nb + b - 1], top)
-            run_max[slot * nb + b] = top
+            slot, b, half = new
+            run_max[slot * nb + b, place(slot, half)[0], :] = top
 
     diagonal = lax.broadcasted_iota(jnp.int32, (128, 128), 0) == lax.broadcasted_iota(
         jnp.int32, (128, 128), 1
@@ -397,16 +397,19 @@
 
         lax.fori_loop(first, last, block, 0)
 
+    mine, other = co, 1 - co
+    step((0, 0, mine), None)
+    step((0, 1, mine), (0, 0, mine))
+    pass_on(2, 1)
     from_partner(2, 0)
-    step((0, 0), None)
-    pass_on(2, 1)
+    step((0, 0, other), (0, 1, mine))
+    step((0, 1, other), (0, 0, other))
     for zp in (0, 1):
         for kind in (0, 1):
             to_partner(kind, zp)
-    step((0, 1), (0, 0))
-    step((0, 2), (0, 1))
-    step((0, 3), (0, 2))
-    step(None, (0, 3))
+    step((0, 2, None), (0, 1, other))
+    step((0, 3, None), (0, 2, None))
+    step(None, (0, 3, None))
     local_stats(0)
     start_near(1)
     for zp in (0, 1):
@@ -419,13 +422,15 @@
     lax.fori_loop(nb // 2, nb, index_block, 0)
     index_stats()
     start_near(0)
+    step((1, 0, mine), None)
+    step((1, 1, mine), (1, 0, mine))
     from_partner(2, 1)
-    step((1, 0), None)
     start_z(1, ATT)
-    step((1, 1), (1, 0))
-    step((1, 2), (1, 1))
-    step((1, 3), (1, 2))
-    step(None, (1, 3))
+    step((1, 0, other), (1, 1, mine))
+    step((1, 1, other), (1, 0, other))
+    step((1, 2, None), (1, 1, other))
+    step((1, 3, None), (1, 2, None))
+    step(None, (1, 3, None))
     local_stats(1)
     earlier = list(sent)
     sent.clear()

time: 51 us -> 50.4 us (0.988)
  Pallas kernels: 49.6 us -> 49 us
    pallas_call x1, Pallas kernels: 49.6 us -> 49 us  [body(): pl.pallas_call(kernel, out_shape=(jax.ShapeDtypeStruct((8, n_keys), f32),...]
where the time goes in v5:
time: 50.4 us; the launch traced here: 50.3 us
  Pallas kernels  49 us (97%)
  other arithmetic  0.72 us (1%)
  between operations  0.64 us (1%)
    pallas_call x1, Pallas kernels, body(): pl.pallas_call(kernel, out_shape=(jax.ShapeDtypeStruct((8, n_keys), f32),...  49 us

profile of v5, /device:TPU:1, one launch (start us, length us, event | category | flops | bytes accessed | tf_op | source)
XLA Modules:
  0.0 50.3 jit_solution(880217716051032241)
XLA Ops:
  0.6 49.0 %scores_to_gradient.1 = (f32[8,4096]{1,0:T(8,128)S(1)}, f32[8,4096]{1,0:T(8,128)S(1)}) custom-call(bf16[2,16,576]{2,1,0:T(8,128)(2,1)} %q_ref.1, bf16[2,8,128]{2,1,0:T(8,128)(2,1)} %iq_ref.1, bf16[2,8]{1,0:T(2,128)(2,1)} %iw_ref.1, bf16[576,4096]{1,0:T(8,128)(2,1)} %bitcast.1, bf16[4096,128]{1,0:T(8,128)(2,1)} %ik_ref.1, s32[64]{0:T(128)} %len_ref.1), custom_call_target="tpu_custom_call" | custom-call | tf_op jit(solution)/shard_map/scores_to_gradient/pallas_call | solution.py:464
  49.6 0.7 %subtract_multiply_fusion = (f32[8,4096]{1,0:T(8,128)}, f32[8,4096]{1,0:T(8,128)}) fusion(f32[8,4096]{1,0:T(8,128)S(1)} %get-tuple-element.5, f32[8,4096]{1,0:T(8,128)S(1)} %get-tuple-element.4), kind=kLoop, calls=%fused_computation | loop fusion | flops 98304 | bytes 524288 | tf_op jit(solution)/shard_map/mul | solution.py:507

commit v6 on v5

--- a/solution.py
+++ b/solution.py
@@ -135,14 +135,21 @@
             copy = remote(
                 (iq_ref, iw_ref, q_ref)[kind],
                 bufs[kind].at[rows_of(kind, c % 4), h],
-                land_send.at[kind, k],
+                land_send.at[k if kind == 1 else 4 + kind // 2],
                 land_recv.at[kind, zl % 2, h // 4, 0],
                 d,
             )
             if start:
                 copy.start()
-            else:
+            elif kind == 1:
                 sent.append(copy)
+        if not start and kind != 1:
+            four = bufs[kind].at[:, 0]
+            sent.append(
+                remote(
+                    four, four, land_send.at[4 + kind // 2], land_recv.at[kind, 0, 0, 0], lands[0]
+                )
+            )
 
     def view_of(kind, zp, zh, k):
         return bufs[kind].at[rows_of(kind, zp * 2 + co), zh * 4 + src_y((x + k) % 4)]
@@ -150,7 +157,7 @@
     def arrived(kind, zp, zh, k):
         view = view_of(kind, zp, zh, k)
         remote(
-            view, view, land_send.at[kind, 0], land_recv.at[kind, zp, zh, k], x_others[0]
+            view, view, land_send.at[0], land_recv.at[kind, zp, zh, k], x_others[0]
         ).wait_recv()
 
     def pass_on(kind, zp):
@@ -162,12 +169,26 @@
                 copy = remote(
                     view,
                     view,
-                    step_send.at[kind, zp, i, step - 1],
+                    step_send.at[
+                        zp * 6 + i * 3 + step - 1 if kind == 1 else 12 + kind + zp
+                    ],
                     land_recv.at[kind, zp, zh, 4 - step],
                     x_others[step - 1],
                 )
                 copy.start()
-                sent.append(copy)
+                if kind == 1:
+                    sent.append(copy)
+        if kind != 1:
+            six = bufs[kind].at[0:4, 0:3]
+            sent.append(
+                remote(
+                    six,
+                    six,
+                    step_send.at[12 + kind + zp],
+                    land_recv.at[kind, zp, 0, 0],
+                    x_others[0],
+                )
+            )
 
     def side_copy(kind, zp, core):
         view = bufs[kind].at[rows_of(kind, zp * 2 + core)]
@@ -216,44 +237,48 @@
         return remote(
             st_own.at[e],
             st_near_in.at[e, back - 1],
-            near_send.at[e, k - 1],
-            near_recv.at[e, back - 1],
+            near_send.at[e],
+            near_recv.at[e],
             near[k - 1],
         )
 
     def start_near(e):
         for k in (4, 5, 2, 3, 6, 7, 1):
-            copy = near_copy(e, k)
-            copy.start()
-            sent.append(copy)
+            near_copy(e, k).start()
+        sent.append(near_all(e))
+
+    def near_all(e):
+        every = st_near_in.at[e]
+        return remote(every, every, near_send.at[e], near_recv.at[e], near[0])
+
+    def z_all(e):
+        every = st_z_in.at[e]
+        return remote(every, every, z_s_send.at[e], z_s_recv.at[e], z_others[0])
 
     def start_z(e, scale):
         parts = [(st_own[e, 0], st_own[e, 1])]
-        for k in range(1, 8):
-            near_copy(e, k).wait_recv()
+        near_all(e).wait_recv()
         for k in range(1, 8):
             parts.append((st_near_in[e, k - 1, 0], st_near_in[e, k - 1, 1]))
         m, s = combine(parts, scale)
         st_near[e, 0] = m
         st_near[e, 1] = s
         for k in (1, 3, 2):
-            copy = z_copy(e, k)
-            copy.start()
-            sent.append(copy)
+            z_copy(e, k).start()
+        sent.append(z_all(e))
 
     def z_copy(e, k):
         return remote(
             st_near.at[e],
             st_z_in.at[e, 3 - k],
-            z_s_send.at[e, k - 1],
-            z_s_recv.at[e, 3 - k],
+            z_s_send.at[e],
+            z_s_recv.at[e],
             z_others[k - 1],
         )
 
     def finish(e, scale):
         parts = [(st_near[e, 0], st_near[e, 1])]
-        for k in (1, 2, 3):
-            z_copy(e, k).wait_recv()
+        z_all(e).wait_recv()
         for k in (1, 2, 3):
             parts.append((st_z_in[e, k - 1, 0], st_z_in[e, k - 1, 1]))
         return combine(parts, scale)
@@ -488,15 +513,15 @@
             pltpu.VMEM((1024, 128), f32),
             *stats,
             dma((2,)),
-            dma((3, 4)),
+            dma((6,)),
             dma((3, 2, 2, 4)),
-            dma((3, 2, 2, 3)),
+            dma((16,)),
             dma((3, 2)),
             dma((3, 2)),
-            dma((3, 7)),
-            dma((3, 7)),
-            dma((3, 3)),
-            dma((3, 3)),
+            dma((3,)),
+            dma((3,)),
+            dma((3,)),
+            dma((3,)),
         ],
         compiler_params=pltpu.CompilerParams(
             collective_id=0, has_side_effects=True, vmem_limit_bytes=36 * 2**20

time: 50.4 us -> 49.7 us (0.986)
  Pallas kernels: 49 us -> 48.3 us
    pallas_call x1, Pallas kernels: 49 us -> 48.3 us  [body(): pl.pallas_call(kernel, out_shape=(jax.ShapeDtypeStruct((8, n_keys), f32),...]
where the time goes in v6:
time: 49.7 us; the launch traced here: 49.6 us
  Pallas kernels  48.3 us (97%)
  other arithmetic  0.72 us (1%)
  between operations  0.64 us (1%)
    pallas_call x1, Pallas kernels, body(): pl.pallas_call(kernel, out_shape=(jax.ShapeDtypeStruct((8, n_keys), f32),...  48.3 us

profile of v6, /device:TPU:1, one launch (start us, length us, event | category | flops | bytes accessed | tf_op | source)
XLA Modules:
  0.0 49.6 jit_solution(16370125048800349457)
XLA Ops:
  0.6 48.3 %scores_to_gradient.1 = (f32[8,4096]{1,0:T(8,128)S(1)}, f32[8,4096]{1,0:T(8,128)S(1)}) custom-call(bf16[2,16,576]{2,1,0:T(8,128)(2,1)} %q_ref.1, bf16[2,8,128]{2,1,0:T(8,128)(2,1)} %iq_ref.1, bf16[2,8]{1,0:T(2,128)(2,1)} %iw_ref.1, bf16[576,4096]{1,0:T(8,128)(2,1)} %bitcast.1, bf16[4096,128]{1,0:T(8,128)(2,1)} %ik_ref.1, s32[64]{0:T(128)} %len_ref.1), custom_call_target="tpu_custom_call" | custom-call | tf_op jit(solution)/shard_map/scores_to_gradient/pallas_call | solution.py:489
  48.9 0.7 %subtract_multiply_fusion = (f32[8,4096]{1,0:T(8,128)}, f32[8,4096]{1,0:T(8,128)}) fusion(f32[8,4096]{1,0:T(8,128)S(1)} %get-tuple-element.5, f32[8,4096]{1,0:T(8,128)S(1)} %get-tuple-element.4), kind=kLoop, calls=%fused_computation | loop fusion | flops 98304 | bytes 524288 | tf_op jit(solution)/shard_map/mul | solution.py:532

commit v7 on v6

--- a/solution.py
+++ b/solution.py
@@ -383,6 +383,7 @@
         m = run_max[slot * nb + nb - 1]
         top = jnp.max(m, axis=1, keepdims=True)
         s = jnp.sum(run_sum[...] * jnp.exp2((m - top) * ATT), axis=1, keepdims=True)
+        lse[slot * SLOT : (slot + 1) * SLOT, :] = jnp.broadcast_to(top * ATT, (SLOT, 128))
         st_own[1 + slot] = jnp.ones((2, 8, 128), jnp.float32)
         for r in range(4):
             part = slice(r * 128, (r + 1) * 128)
@@ -390,15 +391,26 @@
                 line = jnp.sum(jnp.where(diagonal, value[part], 0.0), axis=0, keepdims=True)
                 st_own[1 + slot, plane, r : r + 1, :] = line
 
+    gain = -7.0
+
+    def to_local(slot):
+        rows = slice(slot * SLOT, (slot + 1) * SLOT)
+        for b in range(nb):
+            w = jnp.exp2(run_max[slot * nb + b] * ATT - lse[rows, :])
+            for i in range(nl):
+                at = b * BLOCK + i * 128
+                p_ref[rows, at : at + 128] = p_ref[rows, at : at + 128] * w
+
     def global_stats(slot):
         m, s = finish(1 + slot, ATT)
         both = m * ATT + jnp.log2(s)
         for r in range(4):
             column = jnp.sum(jnp.where(diagonal, both[r : r + 1, :], 0.0), axis=1, keepdims=True)
             at = slot * SLOT + r * 128
-            lse[at : at + 128, :] = jnp.broadcast_to(column, (128, 128))
-
-    gain = -7.0
+            if slot == 0:
+                lse[at : at + 128, :] = jnp.broadcast_to(column, (128, 128))
+            else:
+                lse[at : at + 128, :] = jnp.exp2(lse[at : at + 128, :] - column + gain)
 
     def sweep(slot, first, last):
         def block(b, carry):
@@ -408,9 +420,9 @@
                 for k in range(16):
                     at = r * 128 + k * 8
                     g = slot * SLOT + at
-                    w = jnp.exp2(
-                        run_max[slot * nb + b, at : at + 8, :] * ATT - lse[g : g + 8, :] + gain
-                    )
+                    w = lse[g : g + 8, :]
+                    if slot == 0:
+                        w = jnp.exp2(run_max[b, at : at + 8, :] * ATT - w + gain)
                     for i in range(nl):
                         t = p_ref[g : g + 8, pl.ds(start + i * 128, 128)] * w
                         acc[i] = t if acc[i] is None else acc[i] + t
@@ -466,6 +478,7 @@
     for copy in earlier:
         copy.wait_send()
     start_z(2, ATT)
+    to_local(1)
     m, s = finish(0, LOG2E)
     share = jnp.exp2((st_own[0, 0] - m) * LOG2E) / s
     predicted_ref[...] = logits[...] * share[:, 0:1]

time: 49.7 us -> 49.7 us (level)
  no operation moved by 1% of the time
where the time goes in v7:
time: 49.7 us; the launch traced here: 49.6 us
  Pallas kernels  48.2 us (97%)
  other arithmetic  0.72 us (1%)
  between operations  0.64 us (1%)
    pallas_call x1, Pallas kernels, body(): pl.pallas_call(kernel, out_shape=(jax.ShapeDtypeStruct((8, n_keys), f32),...  48.2 us

profile of v7, /device:TPU:1, one launch (start us, length us, event | category | flops | bytes accessed | tf_op | source)
XLA Modules:
  0.0 49.6 jit_solution(10279102167479267898)
XLA Ops:
  0.6 48.2 %scores_to_gradient.1 = (f32[8,4096]{1,0:T(8,128)S(1)}, f32[8,4096]{1,0:T(8,128)S(1)}) custom-call(bf16[2,16,576]{2,1,0:T(8,128)(2,1)} %q_ref.1, bf16[2,8,128]{2,1,0:T(8,128)(2,1)} %iq_ref.1, bf16[2,8]{1,0:T(2,128)(2,1)} %iw_ref.1, bf16[576,4096]{1,0:T(8,128)(2,1)} %bitcast.1, bf16[4096,128]{1,0:T(8,128)(2,1)} %ik_ref.1, s32[64]{0:T(128)} %len_ref.1), custom_call_target="tpu_custom_call" | custom-call | tf_op jit(solution)/shard_map/scores_to_gradient/pallas_call | solution.py:502
  48.9 0.7 %subtract_multiply_fusion = (f32[8,4096]{1,0:T(8,128)}, f32[8,4096]{1,0:T(8,128)}) fusion(f32[8,4096]{1,0:T(8,128)S(1)} %get-tuple-element.5, f32[8,4096]{1,0:T(8,128)S(1)} %get-tuple-element.4), kind=kLoop, calls=%fused_computation | loop fusion | flops 98304 | bytes 524288 | tf_op jit(solution)/shard_map/mul | solution.py:545

commit v8 on v6

--- a/solution.py
+++ b/solution.py
@@ -160,8 +160,10 @@
             view, view, land_send.at[0], land_recv.at[kind, zp, zh, k], x_others[0]
         ).wait_recv()
 
-    def pass_on(kind, zp):
+    def pass_on(kind, zp, between=None):
         for i in (0, 1):
+            if i == 1 and between is not None:
+                between()
             zh = (h // 4 + i) % 2
             arrived(kind, zp, zh, 0)
             view = view_of(kind, zp, zh, 0)
@@ -214,8 +216,7 @@
         land(kind, True)
     for kind in (0, 1, 2):
         land(kind, False)
-    pass_on(2, 0)
-    pl.when(jnp.logical_not(first))(lambda: land(2, True))
+    pass_on(2, 0, lambda: pl.when(jnp.logical_not(first))(lambda: land(2, True)))
     for zp in (0, 1):
         for kind in (0, 1):
             pass_on(kind, zp)

time: 49.7 us -> 49.4 us (level)
  no operation moved by 1% of the time
where the time goes in v8:
time: 49.4 us; the launch traced here: 49.3 us
  Pallas kernels  47.9 us (97%)
  other arithmetic  0.72 us (1%)
  between operations  0.64 us (1%)
    pallas_call x1, Pallas kernels, body(): pl.pallas_call(kernel, out_shape=(jax.ShapeDtypeStruct((8, n_keys), f32),...  47.9 us

profile of v8, /device:TPU:1, one launch (start us, length us, event | category | flops | bytes accessed | tf_op | source)
XLA Modules:
  0.0 49.3 jit_solution(16527655579869690510)
XLA Ops:
  0.6 47.9 %scores_to_gradient.1 = (f32[8,4096]{1,0:T(8,128)S(1)}, f32[8,4096]{1,0:T(8,128)S(1)}) custom-call(bf16[2,16,576]{2,1,0:T(8,128)(2,1)} %q_ref.1, bf16[2,8,128]{2,1,0:T(8,128)(2,1)} %iq_ref.1, bf16[2,8]{1,0:T(2,128)(2,1)} %iw_ref.1, bf16[576,4096]{1,0:T(8,128)(2,1)} %bitcast.1, bf16[4096,128]{1,0:T(8,128)(2,1)} %ik_ref.1, s32[64]{0:T(128)} %len_ref.1), custom_call_target="tpu_custom_call" | custom-call | tf_op jit(solution)/shard_map/scores_to_gradient/pallas_call | solution.py:490
  48.5 0.7 %subtract_multiply_fusion = (f32[8,4096]{1,0:T(8,128)}, f32[8,4096]{1,0:T(8,128)}) fusion(f32[8,4096]{1,0:T(8,128)S(1)} %get-tuple-element.5, f32[8,4096]{1,0:T(8,128)S(1)} %get-tuple-element.4), kind=kLoop, calls=%fused_computation | loop fusion | flops 98304 | bytes 524288 | tf_op jit(solution)/shard_map/mul | solution.py:533
